TPU v7x, 1024 devices: a whole 4x8x16 slice. The times are simulated.
1024 devices in a mesh: ctx: 128 (over y_lo, z, core), ch: 8 (over y_hi, x).
Axes of the slice: x: 4, y: 8 (y_hi: 2, y_lo: 4; y = y_hi * 4 + y_lo), z: 16, core: 2. Of those that a mesh axis runs over, the one named last changes fastest.
Arguments:
- query: bfloat16 [16384, 8192], P('ctx', 'ch'), may hold values from -6 to 6
- key: bfloat16 [16384, 8192], P('ctx', 'ch'), may hold values from -6 to 6
- value: bfloat16 [16384, 8192], P('ctx', 'ch'), may hold values from -6 to 6
- cotangent: bfloat16 [16384, 8192], P('ctx', 'ch'), may hold values from -6 to 6
- decay: float32 [4, 8192], P(None, 'ch'), may hold values from 0.95 to 1, as said below
- residue: float32 [4, 8192], P(None, 'ch'), may hold values from -3 to 3
- skip: float32 [8192], P('ch'), may hold values from -4 to 4
Outputs:
- output: bfloat16 [16384, 8192], P('ctx', 'ch')
- query_grad: bfloat16 [16384, 8192], P('ctx', 'ch')
- key_grad: bfloat16 [16384, 8192], P('ctx', 'ch')
- value_grad: bfloat16 [16384, 8192], P('ctx', 'ch')
- residue_grad: float32 [4, 8192], P(None, 'ch')
- skip_grad: float32 [8192], P('ch')
Inputs may be any that keep to these rules, and one draw needn't show every extreme that they name: decay lies below 1.
All inputs are finite; a program needn't handle non-finite values.
Results may differ from a plain program's by a relative error of at most 0.0012.
Values sent between devices are 32-bit elements; how exact they have to be, the bound alone decides.
No kernel may reach another device: no remote copies, remote signals or barrier semaphores. Data moves between devices by JAX's collectives and lax.ppermute only.
A program may use at most 32 MiB of HBM per device.

v0:
```python
import math

import jax
import jax.numpy as jnp
from jax import lax
from jax.sharding import PartitionSpec as P

GROUP = 128


def entering(part, axis, combine, identity, reverse):
    count = lax.axis_size(axis)
    place = lax.axis_index(axis)
    ahead = count - 1 - place if reverse else place
    gathered = jax.tree.map(lambda a: lax.all_gather(a, axis), part)
    state = jax.tree.map(lambda a, e: jnp.zeros_like(a) + jnp.asarray(e, a.dtype), part, identity)

    def one(lap, state):
        source = count - 1 - lap if reverse else lap
        return combine(
            state, jax.tree.map(lambda a: lax.dynamic_index_in_dim(a, source, 0, False), gathered)
        )

    return lax.fori_loop(0, ahead, one, state)


def combine_factors(earlier, later):
    return (earlier[0] * later[1] + later[0], earlier[1] * later[1])


def local(query, key, value, cotangent, decay, residue, skip):
    tok_rows = query.shape[0]
    chan_width = query.shape[1]
    block_count = tok_rows // GROUP
    context = lax.axis_size("ctx")
    inner = key.astype(jnp.float32) * value.astype(jnp.float32)
    grad_z = cotangent.astype(jnp.float32) * query.astype(jnp.float32)
    log_decay = jnp.log(decay)
    spread = jnp.sqrt((1.0 - decay) * (1.0 + decay))
    coeffs = residue * spread
    position = jnp.arange(tok_rows, dtype=jnp.float32)
    tail_state = jnp.sum(
        jnp.exp((tok_rows - 1.0 - position)[None, :, None] * log_decay[:, None, :]) * inner[None],
        axis=1,
    )
    head_state = jnp.sum(
        jnp.exp(position[None, :, None] * log_decay[:, None, :]) * grad_z[None], axis=1
    )
    zeros_state = jnp.zeros_like(decay)
    span_decay = jnp.exp(tok_rows * log_decay)
    identity = (zeros_state, jnp.ones_like(decay))
    carry_in = entering((tail_state, span_decay), "ctx", combine_factors, identity, False)[0]
    carry_back = entering((head_state, span_decay), "ctx", combine_factors, identity, True)[0]
    steps_idx = jnp.arange(GROUP)
    lower = (steps_idx[:, None] >= steps_idx[None, :]).astype(jnp.float32)
    upper = lower.T

    def per_mode(totals, mode_data):
        mode_log, mode_coef, mode_in, mode_back = mode_data
        z_total, du_total = totals
        rising = jnp.exp(-position[:, None] * mode_log[None, :])
        falling = jnp.exp(position[:, None] * mode_log[None, :])
        scaled = (rising * inner).reshape(block_count, GROUP, chan_width)
        within = jnp.einsum("ts,bsc->btc", lower, scaled, precision=lax.Precision.HIGHEST)
        block_sums = jnp.sum(scaled, axis=1)
        earlier_sums = jnp.cumsum(block_sums, axis=0) - block_sums
        running = (within + earlier_sums[:, None, :]).reshape(tok_rows, chan_width)
        forward_state = falling * running + falling * jnp.exp(mode_log)[None, :] * mode_in[None, :]
        scaled_back = (falling * grad_z).reshape(block_count, GROUP, chan_width)
        within_back = jnp.einsum("ts,bsc->btc", upper, scaled_back, precision=lax.Precision.HIGHEST)
        back_sums = jnp.sum(scaled_back, axis=1)
        later_sums = jnp.sum(back_sums, axis=0)[None, :] - jnp.cumsum(back_sums, axis=0)
        running_back = (within_back + later_sums[:, None, :]).reshape(tok_rows, chan_width)
        backward_state = (
            rising * running_back
            + jnp.exp((tok_rows - position)[:, None] * mode_log[None, :]) * mode_back[None, :]
        )
        new_totals = (
            z_total + mode_coef[None, :] * forward_state,
            du_total + mode_coef[None, :] * backward_state,
        )
        return (new_totals, jnp.sum(grad_z * forward_state, axis=0))

    start_totals = (
        jnp.zeros((tok_rows, chan_width), jnp.float32),
        jnp.zeros((tok_rows, chan_width), jnp.float32),
    )
    (mixed, back_mixed), residue_terms = lax.scan(
        per_mode, start_totals, (log_decay, coeffs, carry_in, carry_back)
    )
    mixed_z = mixed + skip[None, :] * inner
    inner_grad = back_mixed + skip[None, :] * grad_z
    output = (query.astype(jnp.float32) * mixed_z).astype(jnp.bfloat16)
    query_grad = (cotangent.astype(jnp.float32) * mixed_z).astype(jnp.bfloat16)
    key_grad = (inner_grad * value.astype(jnp.float32)).astype(jnp.bfloat16)
    value_grad = (inner_grad * key.astype(jnp.float32)).astype(jnp.bfloat16)
    residue_local = spread * residue_terms
    skip_local = jnp.sum(grad_z * inner, axis=0)
    residue_sum, skip_sum = lax.psum((residue_local, skip_local), "ctx")
    scale = 1.0 / math.sqrt(tok_rows * context)
    return (output, query_grad, key_grad, value_grad, residue_sum * scale, skip_sum * scale)


def solution(mesh):
    in_specs = (
        P("ctx", "ch"),
        P("ctx", "ch"),
        P("ctx", "ch"),
        P("ctx", "ch"),
        P(None, "ch"),
        P(None, "ch"),
        P("ch"),
    )
    out_specs = (
        P("ctx", "ch"),
        P("ctx", "ch"),
        P("ctx", "ch"),
        P("ctx", "ch"),
        P(None, "ch"),
        P("ch"),
    )
    return jax.shard_map(local, mesh=mesh, in_specs=in_specs, out_specs=out_specs, check_vma=False)
```

profile of v0, /device:TPU:2, one launch (start us, length us, event | category | flops | bytes accessed | tf_op | source)
XLA Modules:
  0.0 1346.3 jit_solution(17073175173946471479)
XLA Ops:
  7.2 1.4 exponential_bitcast_fusion
  8.6 1.4 convert_multiply_fusion.1
  10.0 1.4 multiply_reduce_fusion.1
  12.9 232.1 %all-gather.14.cloned.1.call-done = f32[128,4,1024]{2,1,0:T(4,128)} async-done(((f32[1,4,1024]{2,1,0:T(4,128)}), f32[128,4,1024]{2,1,0:T(4,128)}) %all-gather.14.cloned.1.call-update) | async-done | bytes 2097168 | tf_op jit(solution)/shard_map/all_gather | solution.py:15
  244.9 226.3 %all-gather.10.cloned.1.call-done = f32[128,4,1024]{2,1,0:T(4,128)} async-done(((f32[1,4,1024]{2,1,0:T(4,128)}), f32[128,4,1024]{2,1,0:T(4,128)}) %all-gather.10.cloned.1.call-update) | async-done | bytes 2097168 | tf_op jit(solution)/shard_map/all_gather | solution.py:15
  471.2 98.8 %while.44 = (s32[]{:T(128)}, f32[4,1024]{1,0:T(4,128)S(1)}, s32[]{:T(128)}, f32[128,4,1024]{2,1,0:T(4,128)}, f32[128,4,1024]{2,1,0:T(4,128)}, /*index=5*/s32[]{:T(128)}, s32[]{:T(128)}, s32[]{:T(128)}, s32[]{:T(128)}) while((s32[]{:T(128)}, f32[4,1024]{1,0:T(4,128)S(1)}, s32[]{:T(128)}, f32[128,4,1024]{2,1,0:T(4,128)}, ...), condition=%wide.region_5.6_spmd, body=%wide.region_4.5_spmd.sunk | while | flops 8198 | bytes 65679 | solution.py:24
  472.0 0.8 bitcast_add_fusion.5
  472.8 0.8 bitcast_add_fusion.5
  473.6 0.8 bitcast_add_fusion.5
  474.3 0.8 bitcast_add_fusion.5
  475.1 0.8 bitcast_add_fusion.5
  475.9 0.8 bitcast_add_fusion.5
  476.7 0.8 bitcast_add_fusion.5
  477.4 0.8 bitcast_add_fusion.5
  478.2 0.8 bitcast_add_fusion.5
  481.3 0.8 bitcast_add_fusion.5
  482.1 0.8 bitcast_add_fusion.5
  482.9 0.8 bitcast_add_fusion.5
  483.7 0.8 bitcast_add_fusion.5
  484.5 0.8 bitcast_add_fusion.5
  485.2 0.8 bitcast_add_fusion.5
  486.0 0.8 bitcast_add_fusion.5
  486.8 0.8 bitcast_add_fusion.5
  487.6 0.8 bitcast_add_fusion.5
  488.3 0.8 bitcast_add_fusion.5
  489.1 0.8 bitcast_add_fusion.5
  489.9 0.8 bitcast_add_fusion.5
  490.7 0.8 bitcast_add_fusion.5
  491.5 0.8 bitcast_add_fusion.5
  492.2 0.8 bitcast_add_fusion.5
  493.0 0.8 bitcast_add_fusion.5
  494.6 0.8 bitcast_add_fusion.5
  495.4 0.8 bitcast_add_fusion.5
  496.1 0.8 bitcast_add_fusion.5
  496.9 0.8 bitcast_add_fusion.5
  497.7 0.8 bitcast_add_fusion.5
  498.5 0.8 bitcast_add_fusion.5
  499.2 0.8 bitcast_add_fusion.5
  500.0 0.8 bitcast_add_fusion.5
  500.8 0.8 bitcast_add_fusion.5
  501.6 0.8 bitcast_add_fusion.5
  521.8 0.8 bitcast_add_fusion.5
  524.2 0.8 bitcast_add_fusion.5
  531.2 0.8 bitcast_add_fusion.5
  534.3 0.8 bitcast_add_fusion.5
  535.8 0.8 bitcast_add_fusion.5
  538.2 0.8 bitcast_add_fusion.5
  542.8 0.8 bitcast_add_fusion.5
  549.8 0.8 bitcast_add_fusion.5
  556.9 0.8 bitcast_add_fusion.5
  563.9 0.8 bitcast_add_fusion.5
  567.0 0.8 bitcast_add_fusion.5
  570.1 127.4 %all-gather.12.cloned.1.call-done = f32[128,4,1024]{2,1,0:T(4,128)} async-done(((f32[1,4,1024]{2,1,0:T(4,128)}), f32[128,4,1024]{2,1,0:T(4,128)}) %all-gather.12.cloned.1.call-update) | async-done | bytes 2097168 | tf_op jit(solution)/shard_map/all_gather | solution.py:15
  697.6 9.7 while.45
  697.9 1.0 multiply_reduce_fusion.5
  698.9 1.0 fusion.48
  700.3 1.0 multiply_reduce_fusion.5
  701.3 1.0 fusion.48
  702.7 1.0 multiply_reduce_fusion.5
  703.8 1.0 fusion.48
  705.1 1.0 multiply_reduce_fusion.5
  706.2 1.0 fusion.48
  707.3 1.5 fusion.35
  708.8 629.7 %all-reduce = (f32[4,1024]{1,0:T(4,128)S(1)}, f32[1024]{0:T(1024)S(1)}) all-reduce(f32[4,1024]{1,0:T(4,128)S(1)} %fusion.36, f32[1024]{0:T(1024)S(1)} %get-tuple-element.399), channel_id=1, replica_groups=mesh['ctx'=128,'ch'=8] {'ctx'}, use_global_device_ids=true, to_apply=%region_11.12 | all-reduce | flops 5120 | bytes 40960 | tf_op jit(solution)/shard_map/psum | solution.py:99
  (141 shorter events, 65.1 us)
Async XLA Ops:
  7.2 237.8 %all-gather.14.cloned.1.call-start = ((), (), s32[]{:S(2)}) async-start(), calls=%async_computation.2 | async-start | bytes 2113536 | tf_op jit(solution)/shard_map/all_gather | solution.py:15
  11.3 459.9 %all-gather.10.cloned.1.call-start = ((), (), s32[]{:S(2)}) async-start(), calls=%async_computation | async-start | bytes 2113536 | tf_op jit(solution)/shard_map/all_gather | solution.py:15
  12.1 685.4 %all-gather.12.cloned.1.call-start = ((), (), s32[]{:S(2)}) async-start(), calls=%async_computation.1 | async-start | bytes 2113536 | tf_op jit(solution)/shard_map/all_gather | solution.py:15
  697.5 9.7 copy-start.4
  697.5 9.8 copy-start
  697.5 9.8 copy-start.1
  697.6 9.8 copy-start.2
  697.6 9.8 copy-start.3
  697.6 9.8 copy-start.5
Sparse Core Ops, SparseCore 0:
  11.5 233.4 all-gather.13
  248.3 222.9 all-gather.9
  474.5 222.9 all-gather.11
where the time goes:
time: 1370 us; the launch traced here: 1350 us
  blocking collectives  630 us (46%)
  waiting for transfers between devices  587 us (43%)
  other arithmetic  103 us (8%)
  between operations  13.9 us (1%)
    psum x1, blocking collectives, local(): residue_sum, skip_sum = lax.psum((residue_local, skip_local), 'ctx')  630 us
    all_gather x3, waiting for transfers between devices, entering(): gathered = jax.tree.map(lambda a: lax.all_gather(a, axis), part)  586 us
    add x127, other arithmetic, combine_factors(): return (earlier[0] * later[1] + later[0], earlier[1] * later[1])  95.9 us
  transfers between devices with their start and end apart: 3, of which 3 were waited for; matrix products, arithmetic and copies ran while one was open for 7% of the time, Pallas kernels for 0%

commit v1 on v0

v1 whole, which is shorter than its diff:
```python
import math

import jax
import jax.numpy as jnp
from jax import lax
from jax.experimental import pallas as pl
from jax.experimental.pallas import tpu as pltpu
from jax.sharding import Mesh, PartitionSpec as P

MODES = 4
SEGS = 8
LANES = 128
WIDTH = 256


def shifted(x, amount, row):
    rolled = pltpu.roll(x, amount % SEGS, axis=0)
    inside = row >= amount if amount > 0 else row < SEGS + amount
    return jnp.where(inside, rolled, 0.0)


def segment_scan(x, factor, direction, row):
    total = shifted(x, direction, row)
    step = 1
    while step < SEGS:
        total = total + factor * shifted(total, direction * step, row)
        factor = factor * factor
        step *= 2
    return total


def summarize(
    query, key, value, cotangent, decay, log_decay, coeffs, skip,
    summary, forward, backward, entered, left, inner_buf, grad_buf,
):
    steps = forward.shape[0]
    row = lax.broadcasted_iota(jnp.int32, (SEGS, LANES), 0)
    for block in range(forward.shape[2] // LANES):
        cols = slice(block * LANES, (block + 1) * LANES)
        inner_buf[block] = key[:, cols].astype(jnp.float32) * value[:, cols].astype(jnp.float32)
        grad_buf[block] = cotangent[:, cols].astype(jnp.float32) * query[:, cols].astype(jnp.float32)

        def spread_row(ref, n):
            return jnp.broadcast_to(ref[n : n + 1, cols], (SEGS, LANES))

        a = [spread_row(decay, n) for n in range(MODES)]
        coef = [spread_row(coeffs, n) for n in range(MODES)]
        direct = spread_row(skip, 0)
        state = [jnp.zeros((SEGS, LANES), jnp.float32) for _ in range(MODES)]
        product = [jnp.zeros((SEGS, LANES), jnp.float32) for _ in range(MODES)]
        plain = jnp.zeros((SEGS, LANES), jnp.float32)
        for i in range(steps):
            u = inner_buf[block, pl.ds(i, SEGS, stride=steps), :]
            g = grad_buf[block, pl.ds(i, SEGS, stride=steps), :]
            mixed = direct * u
            plain = plain + g * u
            for n in range(MODES):
                state[n] = a[n] * state[n] + u
                product[n] = product[n] + g * state[n]
                mixed = mixed + coef[n] * state[n]
            forward[i, :, cols] = mixed
        back = [jnp.zeros((SEGS, LANES), jnp.float32) for _ in range(MODES)]
        for i in reversed(range(steps)):
            g = grad_buf[block, pl.ds(i, SEGS, stride=steps), :]
            mixed = direct * g
            for n in range(MODES):
                back[n] = a[n] * back[n] + g
                mixed = mixed + coef[n] * back[n]
            backward[i, :, cols] = mixed
        for n in range(MODES):
            factor = jnp.exp(float(steps) * spread_row(log_decay, n))
            before = segment_scan(state[n], factor, 1, row)
            after = segment_scan(back[n], factor, -1, row)
            entered[n, :, cols] = before
            left[n, :, cols] = after
            summary[n : n + 1, cols] = (factor * before + state[n])[SEGS - 1 :]
            summary[MODES + n : MODES + n + 1, cols] = (factor * after + back[n])[:1]
            summary[2 * MODES + n : 2 * MODES + n + 1, cols] = jnp.sum(
                product[n] + a[n] * back[n] * before, axis=0, keepdims=True
            )
        summary[3 * MODES : 3 * MODES + 1, cols] = jnp.sum(plain, axis=0, keepdims=True)
        summary[3 * MODES + 1 :, cols] = jnp.zeros((MODES - 1, LANES), jnp.float32)


def finish(
    query, key, value, cotangent, decay, log_decay, coeffs, carry_in, carry_back,
    forward, backward, entered, left,
    output, query_grad, key_grad, value_grad, mixed_buf, back_buf,
):
    steps = forward.shape[0]
    row = lax.broadcasted_iota(jnp.int32, (SEGS, LANES), 0).astype(jnp.float32)
    for block in range(forward.shape[2] // LANES):
        cols = slice(block * LANES, (block + 1) * LANES)

        def spread_row(ref, n):
            return jnp.broadcast_to(ref[n : n + 1, cols], (SEGS, LANES))

        a, ahead, behind = [], [], []
        for n in range(MODES):
            a.append(spread_row(decay, n))
            log_a = spread_row(log_decay, n)
            first = spread_row(coeffs, n) * a[n]
            falling = jnp.exp(float(steps) * row * log_a)
            rising = jnp.exp(float(steps) * (SEGS - 1.0 - row) * log_a)
            ahead.append(first * (entered[n, :, cols] + falling * spread_row(carry_in, n)))
            behind.append(first * (left[n, :, cols] + rising * spread_row(carry_back, n)))
        for i in range(steps):
            mixed = forward[i, :, cols]
            for n in range(MODES):
                mixed = mixed + ahead[n]
                ahead[n] = ahead[n] * a[n]
            mixed_buf[block, pl.ds(i, SEGS, stride=steps), :] = mixed
        for i in reversed(range(steps)):
            mixed = backward[i, :, cols]
            for n in range(MODES):
                mixed = mixed + behind[n]
                behind[n] = behind[n] * a[n]
            back_buf[block, pl.ds(i, SEGS, stride=steps), :] = mixed
        mixed_z = mixed_buf[block]
        inner_grad = back_buf[block]
        output[:, cols] = (query[:, cols].astype(jnp.float32) * mixed_z).astype(output.dtype)
        query_grad[:, cols] = (cotangent[:, cols].astype(jnp.float32) * mixed_z).astype(output.dtype)
        key_grad[:, cols] = (inner_grad * value[:, cols].astype(jnp.float32)).astype(output.dtype)
        value_grad[:, cols] = (inner_grad * key[:, cols].astype(jnp.float32)).astype(output.dtype)


def rows_spec(rows):
    return pl.BlockSpec((rows, WIDTH), lambda i: (0, i))


def deep_spec(depth):
    return pl.BlockSpec((depth, SEGS, WIDTH), lambda i: (0, 0, i))


def parts_of(summary):
    return (
        summary[:MODES],
        summary[MODES : 2 * MODES],
        summary[2 * MODES : 3 * MODES],
        summary[3 * MODES : 3 * MODES + 1],
    )


def joined(parts, decay, span):
    tail, head, products, plain = parts[0]
    reach = span
    for later_tail, later_head, later_products, later_plain in parts[1:]:
        products = products + later_products + decay * later_head * tail
        plain = plain + later_plain
        tail = span * tail + later_tail
        head = head + reach * later_head
        reach = reach * span
    return tail, head, products, plain


def around(parts, place, span):
    before = jnp.zeros_like(span)
    after = jnp.zeros_like(span)
    for j in range(len(parts)):
        before = jnp.where(j < place, span * before + parts[j][0], before)
    for j in reversed(range(len(parts))):
        after = jnp.where(j > place, span * after + parts[j][1], after)
    return before, after


def exchanged(summary, axis, size):
    return lax.all_to_all(
        jnp.broadcast_to(summary[None], (size, *summary.shape)), axis, 0, 0, tiled=True
    )


def local(query, key, value, cotangent, decay, residue, skip):
    tokens, width = query.shape
    steps = tokens // SEGS
    log_decay = jnp.log1p(decay - 1.0)
    spread = jnp.sqrt((1.0 - decay) * (1.0 + decay))
    coeffs = residue * spread
    skip_row = skip[None, :]
    grid = (width // WIDTH,)
    wide = rows_spec(tokens)
    modes = rows_spec(MODES)
    shape_of = jax.ShapeDtypeStruct
    f32 = jnp.float32
    summary, forward, backward, entered, left = pl.pallas_call(
        summarize,
        grid=grid,
        in_specs=[wide] * 4 + [modes] * 3 + [rows_spec(1)],
        out_specs=[rows_spec(4 * MODES), deep_spec(steps), deep_spec(steps), deep_spec(MODES), deep_spec(MODES)],
        out_shape=[
            shape_of((4 * MODES, width), f32),
            shape_of((steps, SEGS, width), f32),
            shape_of((steps, SEGS, width), f32),
            shape_of((MODES, SEGS, width), f32),
            shape_of((MODES, SEGS, width), f32),
        ],
        scratch_shapes=[pltpu.VMEM((WIDTH // LANES, tokens, LANES), f32)] * 2,
        name="summarize",
    )(query, key, value, cotangent, decay, log_decay, coeffs, skip_row)

    half = width // 2
    core = lax.axis_index("core")
    pair = lax.all_gather(summary, "core")
    own = lax.dynamic_slice_in_dim(pair, core * half, half, 2)
    own_decay = lax.dynamic_slice_in_dim(decay, core * half, half, 1)
    own_log = lax.dynamic_slice_in_dim(log_decay, core * half, half, 1)
    span = jnp.exp(tokens * own_log)
    stretch = tokens * 2
    stretches = joined([parts_of(own[0]), parts_of(own[1])], own_decay, span)
    inward, outward = jnp.zeros_like(own_log), jnp.zeros_like(own_log)
    reach_in, reach_out = jnp.ones_like(own_log), jnp.ones_like(own_log)
    for axis in ("z_lo", "z_hi", "y"):
        size = lax.axis_size(axis)
        place = lax.axis_index(axis)
        block = jnp.concatenate([*stretches, jnp.zeros((MODES - 1, half), f32)], axis=0)
        everyone = exchanged(block, axis, size)
        parts = [parts_of(everyone[j]) for j in range(size)]
        span = jnp.exp(stretch * own_log)
        before, after = around(parts, place, span)
        inward = inward + reach_in * before
        outward = outward + reach_out * after
        reach_in = reach_in * jnp.exp((stretch * place).astype(f32) * own_log)
        reach_out = reach_out * jnp.exp((stretch * (size - 1 - place)).astype(f32) * own_log)
        stretches = joined(parts, own_decay, span)
        stretch *= size
    _, _, products, plain = stretches
    final = jnp.concatenate([inward, outward, products, plain, jnp.zeros((MODES - 1, half), f32)], axis=0)
    final = lax.all_gather(final, "core", axis=1, tiled=True)
    inward, outward, products, plain = parts_of(final)
    span = jnp.exp(tokens * log_decay)
    first = core == 0
    carry_in = jnp.where(first, inward, pair[0, :MODES] + span * inward)
    carry_back = jnp.where(first, pair[1, MODES : 2 * MODES] + span * outward, outward)

    bf16 = shape_of((tokens, width), query.dtype)
    output, query_grad, key_grad, value_grad = pl.pallas_call(
        finish,
        grid=grid,
        in_specs=[wide] * 4 + [modes] * 5 + [deep_spec(steps), deep_spec(steps), deep_spec(MODES), deep_spec(MODES)],
        out_specs=[wide] * 4,
        out_shape=[bf16] * 4,
        scratch_shapes=[pltpu.VMEM((WIDTH // LANES, tokens, LANES), f32)] * 2,
        name="finish",
    )(query, key, value, cotangent, decay, log_decay, coeffs, carry_in, carry_back, forward, backward, entered, left)
    scale = 1.0 / math.sqrt(tokens * lax.axis_size(("y", "z_hi", "z_lo", "core")))
    return (output, query_grad, key_grad, value_grad, spread * products * scale, plain[0] * scale)


def solution(mesh):
    context = ("y", "z_hi", "z_lo", "core")
    rows, columns = mesh.devices.shape
    fine = Mesh(mesh.devices.reshape(rows // 32, 4, 4, 2, columns), (*context, "ch"))
    wide, modes, flat = P(context, "ch"), P(None, "ch"), P("ch")
    return jax.shard_map(
        local,
        mesh=fine,
        in_specs=(wide, wide, wide, wide, modes, modes, flat),
        out_specs=(wide, wide, wide, wide, modes, flat),
        check_vma=False,
    )
```

time: 1370 us -> 72.6 us (0.05)
  the two profiles are of different devices: /device:TPU:2 before, /device:TPU:1 now
where the time goes in v1:
time: 72.6 us; the launch traced here: 71.9 us
  blocking collectives  50 us (69%)
  Pallas kernels  7.86 us (11%)
  waiting for transfers between devices  4.77 us (7%)
  starting transfers between devices  4.59 us (6%)
  other arithmetic  2.34 us (3%)
  local copies, waits for them, and re-layouts  1.62 us (2%)
  between operations  0.76 us (1%)
    all_to_all x2, blocking collectives, exchanged(): lax.all_to_all(jnp.broadcast_to(summary[None], (size, *summary.shape)), a...  26.6 us
    all_gather x1, blocking collectives, local(): pair = lax.all_gather(summary, 'core')  15.9 us
    all_gather x1, blocking collectives, local(): final = lax.all_gather(final, 'core', axis=1, tiled=True)  7.48 us
    all_to_all x1, waiting for transfers between devices, exchanged(): lax.all_to_all(jnp.broadcast_to(summary[None], (size, *summary.shape)), a...  4.77 us
    all_to_all x1, starting transfers between devices, exchanged(): lax.all_to_all(jnp.broadcast_to(summary[None], (size, *summary.shape)), a...  4.59 us
    pallas_call x1, Pallas kernels, local(): pl.pallas_call(finish, grid=grid, in_specs=[wide] * 4 + [modes] * 5 + [de...  3.94 us
    pallas_call x1, Pallas kernels, local(): pl.pallas_call(summarize, grid=grid, in_specs=[wide] * 4 + [modes] * 3 +...  3.92 us
  transfers between devices with their start and end apart: 1, of which 1 were waited for; matrix products, arithmetic and copies ran while one was open for 0% of the time, Pallas kernels for 0%

profile of v1, /device:TPU:1, one launch (start us, length us, event | category | flops | bytes accessed | tf_op | source)
XLA Modules:
  0.0 71.9 jit_solution(2030424969063571463)
XLA Ops:
  0.6 0.0 copy-start.3
  0.6 0.0 copy-start.1
  0.7 0.7 copy-done.3
  1.4 0.0 copy-done.1
  1.4 0.6 fusion.5
  2.0 3.9 %summarize.1 = (f32[16,1024]{1,0:T(8,128)}, f32[16,8,1024]{2,1,0:T(8,128)}, f32[16,8,1024]{2,1,0:T(8,128)}, f32[4,8,1024]{2,1,0:T(8,128)}, f32[4,8,1024]{2,1,0:T(8,128)}) custom-call(bf16[128,1024]{1,0:T(8,128)(2,1)} %query.3, bf16[128,1024]{1,0:T(8,128)(2,1)} %key.3, bf16[128,1024]{1,0:T(8,128)(2,1)} %value.3, bf16[128,1024]{1,0:T(8,128)(2,1)} %cotangent.3, ...), custom_call_target="tpu_custom_call" | custom-call | tf_op jit(solution)/shard_map/summarize/pallas_call | solution.py:184
  5.9 0.0 copy-start
  5.9 0.0 copy-start.2
  6.0 15.9 %all-gather = f32[32,1024]{1,0:T(8,128)S(1)} all-gather(f32[16,1024]{1,0:T(8,128)} %get-tuple-element.15), channel_id=2, replica_groups=mesh['y'=4,'z_hi'=4,'z_lo'=4,'core'=2,'ch'=8] {'core'}, dimensions={0}, use_global_device_ids=true | all-gather | bytes 196608 | tf_op jit(solution)/shard_map/all_gather | solution.py:202
  21.8 0.1 fusion.45
  21.9 0.0 copy-done
  21.9 0.0 copy-done.2
  21.9 0.1 fusion.40
  22.1 7.3 %all_to_all.15 = f32[4,16,512]{2,1,0:T(8,128)S(1)} all-to-all(f32[4,16,512]{2,1,0:T(8,128)S(1)} %broadcast_in_dim.9), channel_id=1, replica_groups=mesh['y'=4,'z_hi'=4,'z_lo'=4,'core'=2,'ch'=8] {'z_lo'}, dimensions={0} | all-to-all | bytes 262144 | tf_op jit(solution)/shard_map/all_to_all | solution.py:167
  29.5 19.4 %all_to_all.16 = f32[4,16,512]{2,1,0:T(8,128)S(1)} all-to-all(f32[4,16,512]{2,1,0:T(8,128)S(1)} %broadcast_in_dim.10), channel_id=1, replica_groups=mesh['y'=4,'z_hi'=4,'z_lo'=4,'core'=2,'ch'=8] {'z_hi'}, dimensions={0} | all-to-all | bytes 262144 | tf_op jit(solution)/shard_map/all_to_all | solution.py:167
  49.0 0.7 broadcast_in_dim.11
  49.7 4.6 %all-to-all-start.2 = ((f32[4,16,512]{2,1,0:T(8,128)}), f32[4,16,512]{2,1,0:T(8,128)S(1)}, u32[]{:S(2)}, u32[]{:S(2)}) async-start(f32[4,16,512]{2,1,0:T(8,128)} %broadcast_in_dim.11), calls=%async_computation.2 | async-start | bytes 262144 | tf_op jit(solution)/shard_map/all_to_all | solution.py:167
  54.3 4.8 %all-to-all-done.2 = f32[4,16,512]{2,1,0:T(8,128)S(1)} async-done(((f32[4,16,512]{2,1,0:T(8,128)}), f32[4,16,512]{2,1,0:T(8,128)S(1)}, u32[]{:S(2)}, u32[]{:S(2)}) %all-to-all-start.2) | async-done | bytes 131104 | tf_op jit(solution)/shard_map/all_to_all | solution.py:167
  59.1 0.1 fusion.25
  59.1 0.1 fusion.21
  59.3 7.5 %all_gather.11 = f32[16,1024]{1,0:T(8,128)S(1)} all-gather(f32[16,512]{1,0:T(8,128)S(1)} %concatenate.15), channel_id=1, replica_groups=mesh['y'=4,'z_hi'=4,'z_lo'=4,'core'=2,'ch'=8] {'core'}, dimensions={1}, use_global_device_ids=true | all-gather | bytes 98304 | tf_op jit(solution)/shard_map/all_gather | solution.py:227
  66.7 0.6 slice_multiply_fusion.1
  67.3 0.7 fusion.2
  68.0 3.9 %finish.1 = (bf16[128,1024]{1,0:T(8,128)(2,1)}, bf16[128,1024]{1,0:T(8,128)(2,1)}, bf16[128,1024]{1,0:T(8,128)(2,1)}, bf16[128,1024]{1,0:T(8,128)(2,1)}) custom-call(bf16[128,1024]{1,0:T(8,128)(2,1)} %query.3, bf16[128,1024]{1,0:T(8,128)(2,1)} %key.3, bf16[128,1024]{1,0:T(8,128)(2,1)} %value.3, bf16[128,1024]{1,0:T(8,128)(2,1)} %cotangent.3, ...), custom_call_target="tpu_custom_call" | custom-call | tf_op jit(solution)/shard_map/finish/pallas_call | solution.py:235
  (15 shorter events, 0.4 us)
Async XLA Ops:
  0.6 0.7 copy-start.3
  0.6 0.7 %copy-start.1 = (f32[4,1024]{1,0:T(4,128)S(1)}, f32[4,1024]{1,0:T(4,128)}, u32[]{:S(2)}) copy-start(f32[4,1024]{1,0:T(4,128)} %decay.3) | copy-start | bytes 49156
  5.9 16.0 %copy-start = (f32[4,1024]{1,0:T(4,128)S(1)}, f32[4,1024]{1,0:T(4,128)}, u32[]{:S(2)}) copy-start(f32[4,1024]{1,0:T(4,128)} %get-tuple-element.35.log_decay) | copy-start | bytes 49156
  5.9 16.0 %copy-start.2 = (f32[4,1024]{1,0:T(4,128)S(1)}, f32[4,1024]{1,0:T(4,128)}, u32[]{:S(2)}) copy-start(f32[4,1024]{1,0:T(4,128)} %decay.3) | copy-start | bytes 49156
  49.7 9.4 %all-to-all-start.2 = ((f32[4,16,512]{2,1,0:T(8,128)}), f32[4,16,512]{2,1,0:T(8,128)S(1)}, u32[]{:S(2)}, u32[]{:S(2)}) async-start(f32[4,16,512]{2,1,0:T(8,128)} %broadcast_in_dim.11), calls=%async_computation.2 | async-start | bytes 262144 | tf_op jit(solution)/shard_map/all_to_all | solution.py:167

commit v2 on v1

v2 whole, which is shorter than its diff:
```python
import math

import jax
import jax.numpy as jnp
from jax import lax
from jax.experimental import pallas as pl
from jax.experimental.pallas import tpu as pltpu
from jax.sharding import Mesh, PartitionSpec as P

MODES = 4
SEGS = 8
LANES = 128
TOGETHER = 2
MIX_WIDTH = 512
VMEM_LIMIT = 16 * 1024 * 1024


def shifted(x, amount, row):
    rolled = pltpu.roll(x, amount % SEGS, axis=0)
    inside = row >= amount if amount > 0 else row < SEGS + amount
    return jnp.where(inside, rolled, 0.0)


def segment_scan(x, factor, direction, row):
    total = shifted(x, direction, row)
    step = 1
    while step < SEGS:
        total = total + factor * shifted(total, direction * step, row)
        factor = factor * factor
        step *= 2
    return total


def columns(block):
    return pl.ds(pl.multiple_of(block * LANES, LANES), LANES)


def over_blocks(count, one):
    def trip(step, carry):
        for k in range(TOGETHER):
            one(step * TOGETHER + k, k)
        return carry

    lax.fori_loop(0, count // TOGETHER, trip, 0)


def spread_out(ref, n, cols):
    return jnp.broadcast_to(ref[n : n + 1, cols], (SEGS, LANES))


def mode_weights(decay, residue, cols):
    a = [spread_out(decay, n, cols) for n in range(MODES)]
    return a, [spread_out(residue, n, cols) * jnp.sqrt((1.0 - x) * (1.0 + x)) for n, x in enumerate(a)]


def squared(x, times):
    for _ in range(times):
        x = x * x
    return x


def loaded(query, key, value, cotangent, inner_buf, grad_buf, block, cols):
    inner_buf[block] = key[:, cols].astype(jnp.float32) * value[:, cols].astype(jnp.float32)
    grad_buf[block] = cotangent[:, cols].astype(jnp.float32) * query[:, cols].astype(jnp.float32)


def summarize(
    query, key, value, cotangent, decay_away,
    summary, query_held, key_held, value_held, cotangent_held, inner_buf, grad_buf, decay, arrived,
):
    tokens, width = query.shape
    steps = tokens // SEGS
    held = (query_held, key_held, value_held, cotangent_held)
    row = lax.broadcasted_iota(jnp.int32, (SEGS, LANES), 0)
    zero = jnp.zeros((SEGS, LANES), jnp.float32)

    copies = [
        pltpu.make_async_copy(ref, to, arrived.at[n])
        for n, (ref, to) in enumerate(zip((decay_away, query, key, value, cotangent), (decay, *held)))
    ]
    for copy in copies:
        copy.start()
    for copy in copies:
        copy.wait()

    def one(block, buf):
        cols = columns(block)
        loaded(*held, inner_buf, grad_buf, buf, cols)
        a = [spread_out(decay, n, cols) for n in range(MODES)]
        state, back, product, plain = [zero] * MODES, [zero] * MODES, [zero] * MODES, zero
        power = [zero + 1.0] * MODES
        for i in range(steps):
            u = inner_buf[buf, pl.ds(i, SEGS, stride=steps), :]
            g = grad_buf[buf, pl.ds(i, SEGS, stride=steps), :]
            plain = plain + g * u
            for n in range(MODES):
                state[n] = a[n] * state[n] + u
                product[n] = product[n] + g * state[n]
                back[n] = back[n] + power[n] * g
                power[n] = power[n] * a[n]
        for n in range(MODES):
            factor = power[n]
            before = segment_scan(state[n], factor, 1, row)
            after = segment_scan(back[n], factor, -1, row)
            summary[block, n : n + 1] = (factor * before + state[n])[SEGS - 1 :]
            summary[block, MODES + n : MODES + n + 1] = (factor * after + back[n])[:1]
            summary[block, 2 * MODES + n : 2 * MODES + n + 1] = jnp.sum(
                product[n] + a[n] * back[n] * before, axis=0, keepdims=True
            )
        summary[block, 3 * MODES : 3 * MODES + 1] = jnp.sum(plain, axis=0, keepdims=True)
        summary[block, 3 * MODES + 1 :] = jnp.zeros((MODES - 1, LANES), jnp.float32)

    over_blocks(width // LANES, one)


def mix(
    query, key, value, cotangent, decay, residue, skip,
    forward, backward, entered, left, decays, inner_buf, grad_buf,
):
    steps = forward.shape[0]
    doublings = steps.bit_length() - 1
    row = lax.broadcasted_iota(jnp.int32, (SEGS, LANES), 0)
    zero = jnp.zeros((SEGS, LANES), jnp.float32)
    for block in range(forward.shape[2] // LANES):
        cols = slice(block * LANES, (block + 1) * LANES)
        loaded(query, key, value, cotangent, inner_buf, grad_buf, block, cols)
        a, coef = mode_weights(decay, residue, cols)
        direct = spread_out(skip, 0, cols)
        state, back = [zero] * MODES, [zero] * MODES
        for i in range(steps):
            u = inner_buf[block, pl.ds(i, SEGS, stride=steps), :]
            mixed = direct * u
            for n in range(MODES):
                state[n] = a[n] * state[n] + u
                mixed = mixed + coef[n] * state[n]
            forward[i, :, cols] = mixed
        for i in reversed(range(steps)):
            g = grad_buf[block, pl.ds(i, SEGS, stride=steps), :]
            mixed = direct * g
            for n in range(MODES):
                back[n] = a[n] * back[n] + g
                mixed = mixed + coef[n] * back[n]
            backward[i, :, cols] = mixed
        for n in range(MODES):
            factor = squared(a[n], doublings)
            first = coef[n] * a[n]
            entered[n, :, cols] = first * segment_scan(state[n], factor, 1, row)
            left[n, :, cols] = first * segment_scan(back[n], factor, -1, row)
        decays[block] = decay[:, cols]


def finish(
    query, key, value, cotangent, decay, residue, carried,
    forward, backward, entered, left,
    output, query_grad, key_grad, value_grad, residue_grad, skip_grad, mixed_buf, back_buf,
):
    steps = forward.shape[0]
    doublings = steps.bit_length() - 1
    row = lax.broadcasted_iota(jnp.int32, (SEGS, LANES), 0)
    for block in range(forward.shape[2] // LANES):
        cols = slice(block * LANES, (block + 1) * LANES)
        a, coef = mode_weights(decay, residue, cols)
        ahead, behind = [], []
        for n in range(MODES):
            first = coef[n] * a[n]
            factor = squared(a[n], doublings)
            falling, rising = 1.0, 1.0
            for bit in (1, 2, 4):
                falling = falling * jnp.where(row & bit != 0, factor, 1.0)
                rising = rising * jnp.where(row & bit != 0, 1.0, factor)
                factor = factor * factor
            carry_in = jnp.broadcast_to(carried[block, n : n + 1], (SEGS, LANES))
            carry_back = jnp.broadcast_to(carried[block, MODES + n : MODES + n + 1], (SEGS, LANES))
            ahead.append(entered[n, :, cols] + first * falling * carry_in)
            behind.append(left[n, :, cols] + first * rising * carry_back)
        for i in range(steps):
            mixed = forward[i, :, cols]
            for n in range(MODES):
                mixed = mixed + ahead[n]
                ahead[n] = ahead[n] * a[n]
            mixed_buf[block, pl.ds(i, SEGS, stride=steps), :] = mixed
        for i in reversed(range(steps)):
            mixed = backward[i, :, cols]
            for n in range(MODES):
                mixed = mixed + behind[n]
                behind[n] = behind[n] * a[n]
            back_buf[block, pl.ds(i, SEGS, stride=steps), :] = mixed
        mixed_z = mixed_buf[block]
        inner_grad = back_buf[block]
        output[:, cols] = (query[:, cols].astype(jnp.float32) * mixed_z).astype(output.dtype)
        query_grad[:, cols] = (cotangent[:, cols].astype(jnp.float32) * mixed_z).astype(output.dtype)
        key_grad[:, cols] = (inner_grad * value[:, cols].astype(jnp.float32)).astype(output.dtype)
        value_grad[:, cols] = (inner_grad * key[:, cols].astype(jnp.float32)).astype(output.dtype)
        residue_grad[:, cols] = carried[block, 2 * MODES : 3 * MODES]
        skip_grad[:, cols] = carried[block, 3 * MODES : 3 * MODES + 1]


def rows_spec(rows):
    return pl.BlockSpec((rows, MIX_WIDTH), lambda i: (0, i))


def deep_spec(depth):
    return pl.BlockSpec((depth, SEGS, MIX_WIDTH), lambda i: (0, 0, i))


def per_block(rows):
    return pl.BlockSpec((MIX_WIDTH // LANES, rows, LANES), lambda i: (i, 0, 0))


def parts_of(gathered):
    return (
        gathered[:, :MODES],
        gathered[:, MODES : 2 * MODES],
        gathered[:, 2 * MODES : 3 * MODES],
        gathered[:, 3 * MODES : 3 * MODES + 1],
    )


def running(each, spans, reverse):
    step = 1
    for span in spans:
        rest = jnp.zeros((step, *each.shape[1:]), each.dtype)
        moved = jnp.concatenate([each[step:], rest] if reverse else [rest, each[:-step]], axis=0)
        each = each + span * moved
        step *= 2
    return each


def whole_of(parts, decay, spans):
    tails, heads, products, plains = parts
    count = tails.shape[0]
    tail, head, product, plain = tails[0], heads[count - 1], products[0], plains[0]
    for j in range(1, count):
        product = product + products[j] + decay * heads[j] * tail
        plain = plain + plains[j]
        tail = spans[0] * tail + tails[j]
        head = spans[0] * head + heads[count - 1 - j]
    return tail, head, product, plain


def weighted(weights, each):
    total = weights[0] * each[0]
    for j in range(1, each.shape[0]):
        total = total + weights[j] * each[j]
    return total


def padded(parts):
    plain = parts[3]
    rest = jnp.zeros((*plain.shape[:-2], MODES - 1, LANES), plain.dtype)
    return jnp.concatenate([*parts, rest], axis=-2)


def exchanged(blocks, axis):
    return lax.all_to_all(blocks, axis, 0, 0, tiled=True)


def local(query, key, value, cotangent, decay, residue, skip):
    tokens, width = query.shape
    steps = tokens // SEGS
    grid = (width // MIX_WIDTH,)
    wide, modes = rows_spec(tokens), rows_spec(MODES)
    shape_of, f32 = jax.ShapeDtypeStruct, jnp.float32
    buffers = [pltpu.VMEM((MIX_WIDTH // LANES, tokens, LANES), f32)] * 2
    small = pltpu.CompilerParams(vmem_limit_bytes=VMEM_LIMIT)
    far_off, whole = pl.BlockSpec(memory_space=pltpu.HBM), pl.BlockSpec(memory_space=pltpu.VMEM)
    blocks = width // LANES
    away = [pltpu.with_memory_space_constraint(x, pltpu.HBM) for x in (query, key, value, cotangent, decay)]
    summary, *sources = pl.pallas_call(
        summarize,
        in_specs=[far_off] * 5,
        out_specs=[whole] * 5,
        out_shape=[shape_of((blocks, 4 * MODES, LANES), f32)] + [pltpu.VMEM((tokens, width), query.dtype)] * 4,
        scratch_shapes=[pltpu.VMEM((TOGETHER, tokens, LANES), f32)] * 2
        + [pltpu.VMEM((MODES, width), f32), pltpu.SemaphoreType.DMA((5,))],
        compiler_params=small,
        name="summarize",
    )(*away)
    deep = [steps, steps, MODES, MODES]
    forward, backward, entered, left, decays = pl.pallas_call(
        mix,
        grid=grid,
        in_specs=[wide] * 4 + [modes] * 2 + [rows_spec(1)],
        out_specs=[deep_spec(depth) for depth in deep]
        + [per_block(MODES)],
        out_shape=[shape_of((depth, SEGS, width), f32) for depth in deep] + [shape_of((blocks, MODES, LANES), f32)],
        scratch_shapes=buffers,
        compiler_params=small,
        cost_estimate=pl.CostEstimate(flops=40 * tokens * width, bytes_accessed=16 * tokens * width, transcendentals=0),
        name="mix",
    )(*sources, decay, residue, skip[None, :])

    near = ("z_lo", "core")
    own_decay = lax.dynamic_index_in_dim(decays, lax.axis_index(near), 0, False)
    log_decay = jnp.log1p(own_decay - 1.0)

    def power(counts):
        return jnp.exp(counts[:, None, None] * log_decay)

    def held(used, counts):
        return jnp.where(used[:, None, None], power(jnp.maximum(counts, 0).astype(f32)), 0.0)

    near_count = lax.axis_size(near)
    mid_count, far_count = lax.axis_size("z_hi"), lax.axis_size("y")
    mid_place, far_place = lax.axis_index("z_hi"), lax.axis_index("y")
    mid_length = tokens * near_count
    far_length = mid_length * mid_count
    near_place = jnp.arange(near_count)
    reach_in = power((tokens * near_place).astype(f32))
    reach_back = power((tokens * (near_count - 1 - near_place)).astype(f32))
    doublings = (near_count * mid_count * far_count).bit_length() - 1
    spans = power((tokens * (1 << jnp.arange(doublings))).astype(f32))
    near_steps = near_count.bit_length() - 1
    mid_steps = near_steps + mid_count.bit_length() - 1
    mid = jnp.arange(mid_count)
    mid_in = held(mid < mid_place, mid_length * (mid_place - 1 - mid))
    mid_back = held(mid > mid_place, mid_length * (mid - mid_place - 1))
    far = jnp.arange(far_count)
    far_in = held(far < far_place, far_length * (far_place - 1 - far) + mid_length * mid_place)
    far_back = held(far > far_place, far_length * (far - far_place - 1) + mid_length * (mid_count - 1 - mid_place))
    scale = 1.0 / math.sqrt(far_length * far_count)
    spread = jnp.sqrt((1.0 - own_decay) * (1.0 + own_decay)) * scale

    def shared(stretch, count, axis):
        return parts_of(exchanged(jnp.broadcast_to(padded(stretch)[None], (count, 4 * MODES, LANES)), axis))

    near_parts = exchanged(summary, near)
    (
        near_parts, forward, backward, entered, left, own_decay, spread,
        reach_in, reach_back, spans, mid_in, mid_back, far_in, far_back,
    ) = lax.optimization_barrier(
        (
            near_parts, forward, backward, entered, left, own_decay, spread,
            reach_in, reach_back, [spans[k] for k in range(doublings)], mid_in, mid_back, far_in, far_back,
        )
    )
    near_spans, mid_spans, far_spans = spans[:near_steps], spans[near_steps:mid_steps], spans[mid_steps:]
    parts = parts_of(near_parts)
    ahead, behind = running(parts[0], near_spans, False), running(parts[1], near_spans, True)
    rest = jnp.zeros((1, MODES, LANES), f32)
    near_before = jnp.concatenate([rest, ahead[:-1]], axis=0)
    near_after = jnp.concatenate([behind[1:], rest], axis=0)
    products = jnp.sum(parts[2] + own_decay * parts[1] * near_before, axis=0)
    stretch = (ahead[-1], behind[0], products, jnp.sum(parts[3], axis=0))
    near_before, near_after, stretch = lax.optimization_barrier((near_before, near_after, stretch))
    parts = shared(stretch, mid_count, "z_hi")
    entering, leaving = weighted(mid_in, parts[0]), weighted(mid_back, parts[1])
    stretch = whole_of(parts, own_decay, mid_spans)
    entering, leaving, stretch = lax.optimization_barrier((entering, leaving, stretch))
    parts = shared(stretch, far_count, "y")
    entering = entering + weighted(far_in, parts[0])
    leaving = leaving + weighted(far_back, parts[1])
    _, _, products, plain = whole_of(parts, own_decay, far_spans)
    everyone = (near_count, MODES, LANES)
    carried = padded(
        (
            near_before + reach_in * entering,
            near_after + reach_back * leaving,
            jnp.broadcast_to(spread * products, everyone),
            jnp.broadcast_to(scale * plain, (near_count, 1, LANES)),
        )
    )
    carried = exchanged(carried, near)

    bf16 = shape_of((tokens, width), query.dtype)
    *grads, skip_grad = pl.pallas_call(
        finish,
        grid=grid,
        in_specs=[wide] * 4 + [modes] * 2 + [per_block(4 * MODES)] + [deep_spec(depth) for depth in deep],
        out_specs=[wide] * 4 + [modes, rows_spec(1)],
        out_shape=[bf16] * 4 + [shape_of((MODES, width), f32), shape_of((1, width), f32)],
        scratch_shapes=buffers,
        compiler_params=small,
        name="finish",
    )(*sources, decay, residue, carried, forward, backward, entered, left)
    return (*grads, skip_grad[0])


def solution(mesh):
    context = ("y", "z_hi", "z_lo", "core")
    rows, columns = mesh.devices.shape
    fine = Mesh(mesh.devices.reshape(rows // 32, 4, 4, 2, columns), (*context, "ch"))
    wide, modes, flat = P(context, "ch"), P(None, "ch"), P("ch")
    return jax.shard_map(
        local,
        mesh=fine,
        in_specs=(wide, wide, wide, wide, modes, modes, flat),
        out_specs=(wide, wide, wide, wide, modes, flat),
        check_vma=False,
    )
```

time: 72.6 us -> 67.4 us (0.928)
  starting transfers between devices: 4.59 us -> 17.4 us
  blocking collectives: 50 us -> 38.5 us
  waiting for transfers between devices: 4.77 us -> 2.72 us
  Pallas kernels: 7.86 us -> 5.94 us
  other arithmetic: 2.34 us -> 0.51 us
    all_gather x2 -> x0, blocking collectives: 23.3 us -> none  [the longest x1 15.9 us: local(): pair = lax.all_gather(summary, 'core')]
    all_to_all x1, starting transfers between devices: 4.59 us -> 17.4 us  [exchanged(): return lax.all_to_all(blocks, axis, 0, 0, tiled=True)]
    all_to_all x2 -> x3, blocking collectives: 26.6 us -> 38.5 us  [exchanged(): return lax.all_to_all(blocks, axis, 0, 0, tiled=True)]
    all_to_all x1, waiting for transfers between devices: 4.77 us -> 2.72 us  [exchanged(): return lax.all_to_all(blocks, axis, 0, 0, tiled=True)]
    pallas_call x2 -> x3, Pallas kernels: 7.86 us -> 5.94 us  [the longest x1 2.96 us: local(): pl.pallas_call(summarize, in_specs=[far_off] * 5, out_specs=[whole] * 5,...]
    mul x2 -> x4, other arithmetic: 1.25 us -> 0.05 us  [the longest x1 0.02 us: local(): spread = jnp.sqrt((1.0 - own_decay) * (1.0 + own_decay)) * scale]
  transfers between devices with their start and end apart: 1 -> 1, of which waited for: 1 -> 1; matrix products, arithmetic and copies ran while one was open for 0% -> 1% of each run, Pallas kernels for 0% -> 2%
where the time goes in v2:
time: 67.4 us; the launch traced here: 66.9 us
  blocking collectives  38.5 us (57%)
  starting transfers between devices  17.4 us (26%)
  Pallas kernels  5.94 us (9%)
  waiting for transfers between devices  2.72 us (4%)
  between operations  0.94 us (1%)
  local copies, waits for them, and re-layouts  0.91 us (1%)
    all_to_all x3, blocking collectives, exchanged(): return lax.all_to_all(blocks, axis, 0, 0, tiled=True)  38.5 us
    all_to_all x1, starting transfers between devices, exchanged(): return lax.all_to_all(blocks, axis, 0, 0, tiled=True)  17.4 us
    pallas_call x1, Pallas kernels, local(): pl.pallas_call(summarize, in_specs=[far_off] * 5, out_specs=[whole] * 5,...  2.96 us
    all_to_all x1, waiting for transfers between devices, exchanged(): return lax.all_to_all(blocks, axis, 0, 0, tiled=True)  2.72 us
    pallas_call x1, Pallas kernels, local(): pl.pallas_call(finish, grid=grid, in_specs=[wide] * 4 + [modes] * 2 + [pe...  1.77 us
  transfers between devices with their start and end apart: 1, of which 1 were waited for; matrix products, arithmetic and copies ran while one was open for 1% of the time, Pallas kernels for 2%

profile of v2, /device:TPU:1, one launch (start us, length us, event | category | flops | bytes accessed | tf_op | source)
XLA Modules:
  0.0 66.9 jit_solution(5515516280080673622)
XLA Ops:
  0.6 3.0 %summarize.1 = (f32[8,16,128]{2,1,0:T(8,128)}, bf16[128,1024]{1,0:T(8,128)(2,1)S(1)}, bf16[128,1024]{1,0:T(8,128)(2,1)S(1)}, bf16[128,1024]{1,0:T(8,128)(2,1)S(1)}, bf16[128,1024]{1,0:T(8,128)(2,1)S(1)}) custom-call(bf16[128,1024]{1,0:T(8,128)(2,1)} %query.1, bf16[128,1024]{1,0:T(8,128)(2,1)} %key.1, bf16[128,1024]{1,0:T(8,128)(2,1)} %value.1, ...), custom_call_target="tpu_custom_call" | custom-call | tf_op jit(solution)/shard_map/summarize/pallas_call | solution.py:269
  3.6 17.4 %all-to-all-start = ((f32[8,16,128]{2,1,0:T(8,128)}), f32[8,16,128]{2,1,0:T(8,128)S(1)}, u32[]{:S(2)}, u32[]{:S(2)}) async-start(f32[8,16,128]{2,1,0:T(8,128)} %get-tuple-element.56), calls=%async_computation | async-start | bytes 131072 | tf_op jit(solution)/shard_map/all_to_all | solution.py:255
  21.0 0.0 copy-start.2
  21.0 0.0 copy-start
  21.0 0.0 copy-start.1
  21.1 0.6 copy-done.2
  21.7 0.0 copy-done
  21.7 0.0 copy-done.1
  21.7 1.2 %mix.1 = (f32[16,8,1024]{2,1,0:T(8,128)S(1)}, f32[16,8,1024]{2,1,0:T(8,128)S(1)}, f32[4,8,1024]{2,1,0:T(8,128)S(1)}, f32[4,8,1024]{2,1,0:T(8,128)S(1)}, f32[8,4,128]{2,1,0:T(4,128)S(1)}) custom-call(bf16[128,1024]{1,0:T(8,128)(2,1)S(1)} %get-tuple-element.52.query, bf16[128,1024]{1,0:T(8,128)(2,1)S(1)} %get-tuple-element.53.key, ...), custom_call_target="tpu_custom_call" | custom-call | flops 5242880 | bytes 2097152 | tf_op jit(solution)/shard_map/mix/pallas_call | solution.py:280
  23.0 0.1 multiply_exponential_fusion.2
  23.1 0.1 multiply_exponential_fusion
  23.2 0.1 exponential_select_fusion
  23.4 2.7 %all-to-all-done = f32[8,16,128]{2,1,0:T(8,128)S(1)} async-done(((f32[8,16,128]{2,1,0:T(8,128)}), f32[8,16,128]{2,1,0:T(8,128)S(1)}, u32[]{:S(2)}, u32[]{:S(2)}) %all-to-all-start) | async-done | bytes 65568 | tf_op jit(solution)/shard_map/all_to_all | solution.py:255
  26.3 18.4 %all_to_all.20 = f32[4,16,128]{2,1,0:T(8,128)S(1)} all-to-all(f32[4,16,128]{2,1,0:T(8,128)S(1)} %broadcast_in_dim.87), channel_id=1, replica_groups=mesh['y'=4,'z_hi'=4,'z_lo'=4,'core'=2,'ch'=8] {'z_hi'}, dimensions={0} | all-to-all | bytes 65536 | tf_op jit(solution)/shard_map/all_to_all | solution.py:255
  44.9 8.9 %all_to_all.21 = f32[4,16,128]{2,1,0:T(8,128)S(1)} all-to-all(f32[4,16,128]{2,1,0:T(8,128)S(1)} %broadcast_in_dim.88), channel_id=1, replica_groups=mesh['y'=4,'z_hi'=4,'z_lo'=4,'core'=2,'ch'=8] {'y'}, dimensions={0} | all-to-all | bytes 65536 | tf_op jit(solution)/shard_map/all_to_all | solution.py:255
  53.9 0.1 concatenate.43
  53.9 11.2 %all_to_all.22.carried = f32[8,16,128]{2,1,0:T(8,128)S(1)} all-to-all(f32[8,16,128]{2,1,0:T(8,128)S(1)} %concatenate.43), channel_id=1, replica_groups=mesh['y'=4,'z_hi'=4,'z_lo'=4,'core'=2,'ch'=8] {'z_lo','core'}, dimensions={0} | all-to-all | bytes 131072 | tf_op jit(solution)/shard_map/all_to_all | solution.py:255
  65.1 1.8 %finish.1 = (bf16[128,1024]{1,0:T(8,128)(2,1)}, bf16[128,1024]{1,0:T(8,128)(2,1)}, bf16[128,1024]{1,0:T(8,128)(2,1)}, bf16[128,1024]{1,0:T(8,128)(2,1)}, f32[4,1024]{1,0:T(4,128)}, /*index=5*/f32[1,1024]{1,0:T(1,128)}) custom-call(bf16[128,1024]{1,0:T(8,128)(2,1)S(1)} %get-tuple-element.52.query, bf16[128,1024]{1,0:T(8,128)(2,1)S(1)} %get-tuple-element.53.key, ...), custom_call_target="tpu_custom_call" | custom-call | tf_op jit(solution)/shard_map/finish/pallas_call | solution.py:366
  (43 shorter events, 0.4 us)
Async XLA Ops:
  3.6 22.5 %all-to-all-start = ((f32[8,16,128]{2,1,0:T(8,128)}), f32[8,16,128]{2,1,0:T(8,128)S(1)}, u32[]{:S(2)}, u32[]{:S(2)}) async-start(f32[8,16,128]{2,1,0:T(8,128)} %get-tuple-element.56), calls=%async_computation | async-start | bytes 131072 | tf_op jit(solution)/shard_map/all_to_all | solution.py:255
  21.0 0.7 %copy-start.2 = (f32[1024]{0:T(1024)S(1)}, f32[1024]{0:T(1024)}, u32[]{:S(2)}) copy-start(f32[1024]{0:T(1024)} %param.13) | copy-start | bytes 12292
  21.0 0.7 %copy-start = (f32[4,1024]{1,0:T(4,128)S(1)}, f32[4,1024]{1,0:T(4,128)}, u32[]{:S(2)}) copy-start(f32[4,1024]{1,0:T(4,128)} %decay.3) | copy-start | bytes 49156
  21.0 0.7 %copy-start.1 = (f32[4,1024]{1,0:T(4,128)S(1)}, f32[4,1024]{1,0:T(4,128)}, u32[]{:S(2)}) copy-start(f32[4,1024]{1,0:T(4,128)} %residue.3) | copy-start | bytes 49156

commit v3 on v2

--- a/solution.py
+++ b/solution.py
@@ -6,6 +6,7 @@
 from jax.experimental import pallas as pl
 from jax.experimental.pallas import tpu as pltpu
 from jax.sharding import Mesh, PartitionSpec as P
+
 
 MODES = 4
 SEGS = 8
@@ -255,6 +256,22 @@
     return lax.all_to_all(blocks, axis, 0, 0, tiled=True)
 
 
+def swapped(block, place):
+    odd, upper = place % 2 == 1, place >= 2
+    across = lax.ppermute(block, "z_hi", [(2, 0), (3, 1)])
+    wrapped = lax.ppermute(block, "z_hi", [(3, 0), (2, 1)])
+    low = lax.ppermute(block, "z_hi", [(0, 1), (1, 0)])
+    pair = (jnp.where(odd, low, block), jnp.where(odd, block, low))
+    answer = lax.ppermute(jnp.stack(pair), "z_hi", [(0, 2), (1, 3)])
+    high = lax.ppermute(block, "z_hi", [(2, 3), (3, 2)])
+    return [
+        jnp.where(upper, answer[0], pair[0]),
+        jnp.where(upper, answer[1], pair[1]),
+        jnp.where(upper, jnp.where(odd, high, block), jnp.where(odd, wrapped, across)),
+        jnp.where(upper, jnp.where(odd, block, high), jnp.where(odd, across, wrapped)),
+    ]
+
+
 def local(query, key, value, cotangent, decay, residue, skip):
     tokens, width = query.shape
     steps = tokens // SEGS
@@ -343,7 +360,7 @@
     products = jnp.sum(parts[2] + own_decay * parts[1] * near_before, axis=0)
     stretch = (ahead[-1], behind[0], products, jnp.sum(parts[3], axis=0))
     near_before, near_after, stretch = lax.optimization_barrier((near_before, near_after, stretch))
-    parts = shared(stretch, mid_count, "z_hi")
+    parts = parts_of(jnp.stack(swapped(padded(stretch), mid_place)))
     entering, leaving = weighted(mid_in, parts[0]), weighted(mid_back, parts[1])
     stretch = whole_of(parts, own_decay, mid_spans)
     entering, leaving, stretch = lax.optimization_barrier((entering, leaving, stretch))

time: 67.4 us -> 74.4 us (1.10)
  waiting for transfers between devices: 2.72 us -> 22.3 us
  blocking collectives: 38.5 us -> 19.2 us
  starting transfers between devices: 17.4 us -> 23.9 us
    ppermute x0 -> x5, waiting for transfers between devices: none -> 19.6 us  [the longest x1 8.3 us: swapped(): across = lax.ppermute(block, 'z_hi', [(2, 0), (3, 1)])]
    all_to_all x3 -> x2, blocking collectives: 38.5 us -> 19.2 us  [exchanged(): return lax.all_to_all(blocks, axis, 0, 0, tiled=True)]
    ppermute x0 -> x5, starting transfers between devices: none -> 6.51 us  [the longest x1 1.98 us: swapped(): low = lax.ppermute(block, 'z_hi', [(0, 1), (1, 0)])]
  transfers between devices with their start and end apart: 1 -> 6, of which waited for: 1 -> 4; matrix products, arithmetic and copies ran while one was open for 1% -> 0% of each run, Pallas kernels for 2% -> 2%
where the time goes in v3:
time: 74.4 us; the launch traced here: 73.8 us
  starting transfers between devices  23.9 us (32%)
  waiting for transfers between devices  22.3 us (30%)
  blocking collectives  19.2 us (26%)
  Pallas kernels  5.94 us (8%)
  between operations  1.02 us (1%)
  local copies, waits for them, and re-layouts  0.91 us (1%)
    all_to_all x2, blocking collectives, exchanged(): return lax.all_to_all(blocks, axis, 0, 0, tiled=True)  19.2 us
    all_to_all x1, starting transfers between devices, exchanged(): return lax.all_to_all(blocks, axis, 0, 0, tiled=True)  17.4 us
    ppermute x1, waiting for transfers between devices, swapped(): across = lax.ppermute(block, 'z_hi', [(2, 0), (3, 1)])  8.3 us
    ppermute x1, waiting for transfers between devices, swapped(): low = lax.ppermute(block, 'z_hi', [(0, 1), (1, 0)])  6.29 us
    ppermute x1, waiting for transfers between devices, swapped(): wrapped = lax.ppermute(block, 'z_hi', [(3, 0), (2, 1)])  5.03 us
    pallas_call x1, Pallas kernels, local(): pl.pallas_call(summarize, in_specs=[far_off] * 5, out_specs=[whole] * 5,...  2.96 us
    all_to_all x1, waiting for transfers between devices, exchanged(): return lax.all_to_all(blocks, axis, 0, 0, tiled=True)  2.72 us
    ppermute x1, starting transfers between devices, swapped(): low = lax.ppermute(block, 'z_hi', [(0, 1), (1, 0)])  1.98 us
  transfers between devices with their start and end apart: 6, of which 4 were waited for; matrix products, arithmetic and copies ran while one was open for 0% of the time, Pallas kernels for 2%

profile of v3, /device:TPU:1, one launch (start us, length us, event | category | flops | bytes accessed | tf_op | source)
XLA Modules:
  0.0 73.8 jit_solution(17852964577812267986)
XLA Ops:
  0.6 3.0 %summarize.1 = (f32[8,16,128]{2,1,0:T(8,128)}, bf16[128,1024]{1,0:T(8,128)(2,1)S(1)}, bf16[128,1024]{1,0:T(8,128)(2,1)S(1)}, bf16[128,1024]{1,0:T(8,128)(2,1)S(1)}, bf16[128,1024]{1,0:T(8,128)(2,1)S(1)}) custom-call(bf16[128,1024]{1,0:T(8,128)(2,1)} %query.1, bf16[128,1024]{1,0:T(8,128)(2,1)} %key.1, bf16[128,1024]{1,0:T(8,128)(2,1)} %value.1, ...), custom_call_target="tpu_custom_call" | custom-call | tf_op jit(solution)/shard_map/summarize/pallas_call | solution.py:286
  3.6 17.4 %all-to-all-start = ((f32[8,16,128]{2,1,0:T(8,128)}), f32[8,16,128]{2,1,0:T(8,128)S(1)}, u32[]{:S(2)}, u32[]{:S(2)}) async-start(f32[8,16,128]{2,1,0:T(8,128)} %get-tuple-element.56), calls=%async_computation | async-start | bytes 131072 | tf_op jit(solution)/shard_map/all_to_all | solution.py:256
  21.0 0.0 copy-start.2
  21.0 0.0 copy-start
  21.0 0.0 copy-start.1
  21.1 0.6 copy-done.2
  21.7 0.0 copy-done
  21.7 0.0 copy-done.1
  21.7 1.2 %mix.1 = (f32[16,8,1024]{2,1,0:T(8,128)S(1)}, f32[16,8,1024]{2,1,0:T(8,128)S(1)}, f32[4,8,1024]{2,1,0:T(8,128)S(1)}, f32[4,8,1024]{2,1,0:T(8,128)S(1)}, f32[8,4,128]{2,1,0:T(4,128)S(1)}) custom-call(bf16[128,1024]{1,0:T(8,128)(2,1)S(1)} %get-tuple-element.52.query, bf16[128,1024]{1,0:T(8,128)(2,1)S(1)} %get-tuple-element.53.key, ...), custom_call_target="tpu_custom_call" | custom-call | flops 5242880 | bytes 2097152 | tf_op jit(solution)/shard_map/mix/pallas_call | solution.py:297
  23.0 0.1 multiply_exponential_fusion.2
  23.1 0.1 multiply_exponential_fusion
  23.2 0.1 exponential_select_fusion
  23.4 2.7 %all-to-all-done = f32[8,16,128]{2,1,0:T(8,128)S(1)} async-done(((f32[8,16,128]{2,1,0:T(8,128)}), f32[8,16,128]{2,1,0:T(8,128)S(1)}, u32[]{:S(2)}, u32[]{:S(2)}) %all-to-all-start) | async-done | bytes 65568 | tf_op jit(solution)/shard_map/all_to_all | solution.py:256
  26.3 2.0 %collective-permute-start = (f32[16,128]{1,0:T(8,128)S(1)}, f32[16,128]{1,0:T(8,128)S(1)}, u32[]{:S(2)}, u32[]{:S(2)}) collective-permute-start(f32[16,128]{1,0:T(8,128)S(1)} %concatenate.41), channel_id=1, source_target_pairs={{0,64},{64,0},{1,65},{65,1},{2,66},{66,2},{3,67},{67,3},{4,68},{68... | collective-permute-start | bytes 24584 | tf_op jit(solution)/shard_map/ppermute | solution.py:263
  28.3 6.3 %collective-permute-done = f32[16,128]{1,0:T(8,128)S(1)} collective-permute-done((f32[16,128]{1,0:T(8,128)S(1)}, f32[16,128]{1,0:T(8,128)S(1)}, u32[]{:S(2)}, u32[]{:S(2)}) %collective-permute-start) | collective-permute-done | bytes 8224 | tf_op jit(solution)/shard_map/ppermute | solution.py:263
  34.6 1.3 %collective-permute-start.1 = (f32[2,16,128]{2,1,0:T(8,128)S(1)}, f32[2,16,128]{2,1,0:T(8,128)S(1)}, u32[]{:S(2)}, u32[]{:S(2)}) collective-permute-start(f32[2,16,128]{2,1,0:T(8,128)S(1)} %pad_maximum_fusion), channel_id=1, source_target_pairs={{0,128},{64,192},{1,129},{65,193},{2,130},{66,194},{3,131},{67,195... | collective-permute-start | bytes 49160 | tf_op jit(solution)/shard_map/ppermute | solution.py:265
  35.9 1.3 %collective-permute-start.3 = (f32[16,128]{1,0:T(8,128)S(1)}, f32[16,128]{1,0:T(8,128)S(1)}, u32[]{:S(2)}, u32[]{:S(2)}) collective-permute-start(f32[16,128]{1,0:T(8,128)S(1)} %concatenate.41), channel_id=1, source_target_pairs={{192,0},{128,64},{193,1},{129,65},{194,2},{130,66},{195,3},{131,67... | collective-permute-start | bytes 24584 | tf_op jit(solution)/shard_map/ppermute | solution.py:262
  37.2 0.7 collective-permute-start.2
  37.9 1.3 %collective-permute-start.4 = (f32[16,128]{1,0:T(8,128)S(1)}, f32[16,128]{1,0:T(8,128)S(1)}, u32[]{:S(2)}, u32[]{:S(2)}) collective-permute-start(f32[16,128]{1,0:T(8,128)S(1)} %concatenate.41), channel_id=1, source_target_pairs={{128,0},{192,64},{129,1},{193,65},{130,2},{194,66},{131,3},{195,67... | collective-permute-start | bytes 24584 | tf_op jit(solution)/shard_map/ppermute | solution.py:261
  39.2 5.0 %collective-permute-done.3 = f32[16,128]{1,0:T(8,128)S(1)} collective-permute-done((f32[16,128]{1,0:T(8,128)S(1)}, f32[16,128]{1,0:T(8,128)S(1)}, u32[]{:S(2)}, u32[]{:S(2)}) %collective-permute-start.3) | collective-permute-done | bytes 8224 | tf_op jit(solution)/shard_map/ppermute | solution.py:262
  44.2 0.0 collective-permute-done.2
  44.2 8.3 %collective-permute-done.4 = f32[16,128]{1,0:T(8,128)S(1)} collective-permute-done((f32[16,128]{1,0:T(8,128)S(1)}, f32[16,128]{1,0:T(8,128)S(1)}, u32[]{:S(2)}, u32[]{:S(2)}) %collective-permute-start.4) | collective-permute-done | bytes 8224 | tf_op jit(solution)/shard_map/ppermute | solution.py:261
  52.5 0.0 collective-permute-done.1
  52.7 7.8 %all_to_all.15 = f32[4,16,128]{2,1,0:T(8,128)S(1)} all-to-all(f32[4,16,128]{2,1,0:T(8,128)S(1)} %broadcast_in_dim.81), channel_id=1, replica_groups=mesh['y'=4,'z_hi'=4,'z_lo'=4,'core'=2,'ch'=8] {'y'}, dimensions={0} | all-to-all | bytes 65536 | tf_op jit(solution)/shard_map/all_to_all | solution.py:256
  60.6 0.1 concatenate.43
  60.7 11.3 %all_to_all.16.carried = f32[8,16,128]{2,1,0:T(8,128)S(1)} all-to-all(f32[8,16,128]{2,1,0:T(8,128)S(1)} %concatenate.43), channel_id=1, replica_groups=mesh['y'=4,'z_hi'=4,'z_lo'=4,'core'=2,'ch'=8] {'z_lo','core'}, dimensions={0} | all-to-all | bytes 131072 | tf_op jit(solution)/shard_map/all_to_all | solution.py:256
  72.0 1.8 %finish.1 = (bf16[128,1024]{1,0:T(8,128)(2,1)}, bf16[128,1024]{1,0:T(8,128)(2,1)}, bf16[128,1024]{1,0:T(8,128)(2,1)}, bf16[128,1024]{1,0:T(8,128)(2,1)}, f32[4,1024]{1,0:T(4,128)}, /*index=5*/f32[1,1024]{1,0:T(1,128)}) custom-call(bf16[128,1024]{1,0:T(8,128)(2,1)S(1)} %get-tuple-element.52.query, bf16[128,1024]{1,0:T(8,128)(2,1)S(1)} %get-tuple-element.53.key, ...), custom_call_target="tpu_custom_call" | custom-call | tf_op jit(solution)/shard_map/finish/pallas_call | solution.py:383
  (45 shorter events, 0.4 us)
Async XLA Ops:
  3.6 22.5 %all-to-all-start = ((f32[8,16,128]{2,1,0:T(8,128)}), f32[8,16,128]{2,1,0:T(8,128)S(1)}, u32[]{:S(2)}, u32[]{:S(2)}) async-start(f32[8,16,128]{2,1,0:T(8,128)} %get-tuple-element.56), calls=%async_computation | async-start | bytes 131072 | tf_op jit(solution)/shard_map/all_to_all | solution.py:256
  21.0 0.7 copy-start.2
  21.0 0.7 copy-start
  21.0 0.7 copy-start.1
  26.3 8.3 %collective-permute-start = (f32[16,128]{1,0:T(8,128)S(1)}, f32[16,128]{1,0:T(8,128)S(1)}, u32[]{:S(2)}, u32[]{:S(2)}) collective-permute-start(f32[16,128]{1,0:T(8,128)S(1)} %concatenate.41), channel_id=1, source_target_pairs={{0,64},{64,0},{1,65},{65,1},{2,66},{66,2},{3,67},{67,3},{4,68},{68... | collective-permute-start | bytes 24584 | tf_op jit(solution)/shard_map/ppermute | solution.py:263
  34.6 17.9 %collective-permute-start.1 = (f32[2,16,128]{2,1,0:T(8,128)S(1)}, f32[2,16,128]{2,1,0:T(8,128)S(1)}, u32[]{:S(2)}, u32[]{:S(2)}) collective-permute-start(f32[2,16,128]{2,1,0:T(8,128)S(1)} %pad_maximum_fusion), channel_id=1, source_target_pairs={{0,128},{64,192},{1,129},{65,193},{2,130},{66,194},{3,131},{67,195... | collective-permute-start | bytes 49160 | tf_op jit(solution)/shard_map/ppermute | solution.py:265
  35.9 8.3 %collective-permute-start.3 = (f32[16,128]{1,0:T(8,128)S(1)}, f32[16,128]{1,0:T(8,128)S(1)}, u32[]{:S(2)}, u32[]{:S(2)}) collective-permute-start(f32[16,128]{1,0:T(8,128)S(1)} %concatenate.41), channel_id=1, source_target_pairs={{192,0},{128,64},{193,1},{129,65},{194,2},{130,66},{195,3},{131,67... | collective-permute-start | bytes 24584 | tf_op jit(solution)/shard_map/ppermute | solution.py:262
  37.2 7.0 %collective-permute-start.2 = (f32[16,128]{1,0:T(8,128)S(1)}, f32[16,128]{1,0:T(8,128)S(1)}, u32[]{:S(2)}, u32[]{:S(2)}) collective-permute-start(f32[16,128]{1,0:T(8,128)S(1)} %concatenate.41), channel_id=1, source_target_pairs={{128,192},{192,128},{129,193},{193,129},{130,194},{194,130},{131,1... | collective-permute-start | bytes 24584 | tf_op jit(solution)/shard_map/ppermute | solution.py:266
  37.9 14.6 %collective-permute-start.4 = (f32[16,128]{1,0:T(8,128)S(1)}, f32[16,128]{1,0:T(8,128)S(1)}, u32[]{:S(2)}, u32[]{:S(2)}) collective-permute-start(f32[16,128]{1,0:T(8,128)S(1)} %concatenate.41), channel_id=1, source_target_pairs={{128,0},{192,64},{129,1},{193,65},{130,2},{194,66},{131,3},{195,67... | collective-permute-start | bytes 24584 | tf_op jit(solution)/shard_map/ppermute | solution.py:261

commit v4 on v3

--- a/solution.py
+++ b/solution.py
@@ -252,8 +252,9 @@
     return jnp.concatenate([*parts, rest], axis=-2)
 
 
-def exchanged(blocks, axis):
-    return lax.all_to_all(blocks, axis, 0, 0, tiled=True)
+def exchanged(blocks, axis, backwards=False):
+    groups = [list(reversed(range(blocks.shape[0])))] if backwards else None
+    return lax.all_to_all(blocks, axis, 0, 0, tiled=True, axis_index_groups=groups)
 
 
 def swapped(block, place):
@@ -308,7 +309,8 @@
     )(*sources, decay, residue, skip[None, :])
 
     near = ("z_lo", "core")
-    own_decay = lax.dynamic_index_in_dim(decays, lax.axis_index(near), 0, False)
+    near_count = lax.axis_size(near)
+    own_decay = lax.dynamic_index_in_dim(decays, near_count - 1 - lax.axis_index(near), 0, False)
     log_decay = jnp.log1p(own_decay - 1.0)
 
     def power(counts):
@@ -317,14 +319,13 @@
     def held(used, counts):
         return jnp.where(used[:, None, None], power(jnp.maximum(counts, 0).astype(f32)), 0.0)
 
-    near_count = lax.axis_size(near)
     mid_count, far_count = lax.axis_size("z_hi"), lax.axis_size("y")
     mid_place, far_place = lax.axis_index("z_hi"), lax.axis_index("y")
     mid_length = tokens * near_count
     far_length = mid_length * mid_count
     near_place = jnp.arange(near_count)
-    reach_in = power((tokens * near_place).astype(f32))
-    reach_back = power((tokens * (near_count - 1 - near_place)).astype(f32))
+    reach_in = power((tokens * (near_count - 1 - near_place)).astype(f32))
+    reach_back = power((tokens * near_place).astype(f32))
     doublings = (near_count * mid_count * far_count).bit_length() - 1
     spans = power((tokens * (1 << jnp.arange(doublings))).astype(f32))
     near_steps = near_count.bit_length() - 1
@@ -339,9 +340,10 @@
     spread = jnp.sqrt((1.0 - own_decay) * (1.0 + own_decay)) * scale
 
     def shared(stretch, count, axis):
-        return parts_of(exchanged(jnp.broadcast_to(padded(stretch)[None], (count, 4 * MODES, LANES)), axis))
-
-    near_parts = exchanged(summary, near)
+        blocks = jnp.broadcast_to(padded(stretch)[None], (count, 4 * MODES, LANES))
+        return parts_of(exchanged(blocks, axis, backwards=True)[::-1])
+
+    near_parts = exchanged(summary, near, backwards=True)
     (
         near_parts, forward, backward, entered, left, own_decay, spread,
         reach_in, reach_back, spans, mid_in, mid_back, far_in, far_back,
@@ -353,12 +355,12 @@
     )
     near_spans, mid_spans, far_spans = spans[:near_steps], spans[near_steps:mid_steps], spans[mid_steps:]
     parts = parts_of(near_parts)
-    ahead, behind = running(parts[0], near_spans, False), running(parts[1], near_spans, True)
+    ahead, behind = running(parts[0], near_spans, True), running(parts[1], near_spans, False)
     rest = jnp.zeros((1, MODES, LANES), f32)
-    near_before = jnp.concatenate([rest, ahead[:-1]], axis=0)
-    near_after = jnp.concatenate([behind[1:], rest], axis=0)
+    near_before = jnp.concatenate([ahead[1:], rest], axis=0)
+    near_after = jnp.concatenate([rest, behind[:-1]], axis=0)
     products = jnp.sum(parts[2] + own_decay * parts[1] * near_before, axis=0)
-    stretch = (ahead[-1], behind[0], products, jnp.sum(parts[3], axis=0))
+    stretch = (ahead[0], behind[-1], products, jnp.sum(parts[3], axis=0))
     near_before, near_after, stretch = lax.optimization_barrier((near_before, near_after, stretch))
     parts = parts_of(jnp.stack(swapped(padded(stretch), mid_place)))
     entering, leaving = weighted(mid_in, parts[0]), weighted(mid_back, parts[1])
@@ -377,7 +379,7 @@
             jnp.broadcast_to(scale * plain, (near_count, 1, LANES)),
         )
     )
-    carried = exchanged(carried, near)
+    carried = exchanged(carried, near, backwards=True)
 
     bf16 = shape_of((tokens, width), query.dtype)
     *grads, skip_grad = pl.pallas_call(

time: 74.4 us -> 71.6 us (0.962)
  waiting for transfers between devices: 22.3 us -> 20.1 us
  blocking collectives: 19.2 us -> 17.5 us
  starting transfers between devices: 23.9 us -> 25 us
    all_to_all x1, waiting for transfers between devices: 2.72 us -> 0.4 us  [exchanged(): lax.all_to_all(blocks, axis, 0, 0, tiled=True, axis_index_groups=groups)]
    all_to_all x2, blocking collectives: 19.2 us -> 17.5 us  [exchanged(): lax.all_to_all(blocks, axis, 0, 0, tiled=True, axis_index_groups=groups)]
    all_to_all x1, starting transfers between devices: 17.4 us -> 18.5 us  [exchanged(): lax.all_to_all(blocks, axis, 0, 0, tiled=True, axis_index_groups=groups)]
where the time goes in v4:
time: 71.6 us; the launch traced here: 71 us
  starting transfers between devices  25 us (35%)
  waiting for transfers between devices  20.1 us (28%)
  blocking collectives  17.5 us (24%)
  Pallas kernels  5.94 us (8%)
  between operations  1.02 us (1%)
  local copies, waits for them, and re-layouts  0.92 us (1%)
    all_to_all x1, starting transfers between devices, exchanged(): lax.all_to_all(blocks, axis, 0, 0, tiled=True, axis_index_groups=groups)  18.5 us
    all_to_all x2, blocking collectives, exchanged(): lax.all_to_all(blocks, axis, 0, 0, tiled=True, axis_index_groups=groups)  17.5 us
    ppermute x1, waiting for transfers between devices, swapped(): across = lax.ppermute(block, 'z_hi', [(2, 0), (3, 1)])  8.3 us
    ppermute x1, waiting for transfers between devices, swapped(): low = lax.ppermute(block, 'z_hi', [(0, 1), (1, 0)])  6.36 us
    ppermute x1, waiting for transfers between devices, swapped(): wrapped = lax.ppermute(block, 'z_hi', [(3, 0), (2, 1)])  5.03 us
    pallas_call x1, Pallas kernels, local(): pl.pallas_call(summarize, in_specs=[far_off] * 5, out_specs=[whole] * 5,...  2.96 us
    ppermute x1, starting transfers between devices, swapped(): low = lax.ppermute(block, 'z_hi', [(0, 1), (1, 0)])  1.91 us
    pallas_call x1, Pallas kernels, local(): pl.pallas_call(finish, grid=grid, in_specs=[wide] * 4 + [modes] * 2 + [pe...  1.77 us
  transfers between devices with their start and end apart: 6, of which 4 were waited for; matrix products, arithmetic and copies ran while one was open for 0% of the time, Pallas kernels for 2%

profile of v4, /device:TPU:1, one launch (start us, length us, event | category | flops | bytes accessed | tf_op | source)
XLA Modules:
  0.0 71.0 jit_solution(11089346802316799121)
XLA Ops:
  0.6 3.0 %summarize.1 = (f32[8,16,128]{2,1,0:T(8,128)}, bf16[128,1024]{1,0:T(8,128)(2,1)S(1)}, bf16[128,1024]{1,0:T(8,128)(2,1)S(1)}, bf16[128,1024]{1,0:T(8,128)(2,1)S(1)}, bf16[128,1024]{1,0:T(8,128)(2,1)S(1)}) custom-call(bf16[128,1024]{1,0:T(8,128)(2,1)} %query.1, bf16[128,1024]{1,0:T(8,128)(2,1)} %key.1, bf16[128,1024]{1,0:T(8,128)(2,1)} %value.1, ...), custom_call_target="tpu_custom_call" | custom-call | tf_op jit(solution)/shard_map/summarize/pallas_call | solution.py:287
  3.6 18.5 %all-to-all-start = ((f32[8,16,128]{2,1,0:T(8,128)}), f32[8,16,128]{2,1,0:T(8,128)S(1)}, u32[]{:S(2)}, u32[]{:S(2)}) async-start(f32[8,16,128]{2,1,0:T(8,128)} %get-tuple-element.56), calls=%async_computation | async-start | bytes 131072 | tf_op jit(solution)/shard_map/all_to_all | solution.py:257
  22.2 0.0 copy-start.2
  22.2 0.0 copy-start
  22.2 0.0 copy-start.1
  22.2 0.6 copy-done.2
  22.9 0.1 copy-done
  22.9 0.0 copy-done.1
  22.9 1.2 %mix.1 = (f32[16,8,1024]{2,1,0:T(8,128)S(1)}, f32[16,8,1024]{2,1,0:T(8,128)S(1)}, f32[4,8,1024]{2,1,0:T(8,128)S(1)}, f32[4,8,1024]{2,1,0:T(8,128)S(1)}, f32[8,4,128]{2,1,0:T(4,128)S(1)}) custom-call(bf16[128,1024]{1,0:T(8,128)(2,1)S(1)} %get-tuple-element.52.query, bf16[128,1024]{1,0:T(8,128)(2,1)S(1)} %get-tuple-element.53.key, ...), custom_call_target="tpu_custom_call" | custom-call | flops 5242880 | bytes 2097152 | tf_op jit(solution)/shard_map/mix/pallas_call | solution.py:298
  24.2 0.1 multiply_exponential_fusion.2
  24.3 0.1 multiply_exponential_fusion
  24.4 0.1 exponential_select_fusion
  24.5 0.4 all-to-all-done
  25.2 1.9 %collective-permute-start = (f32[16,128]{1,0:T(8,128)S(1)}, f32[16,128]{1,0:T(8,128)S(1)}, u32[]{:S(2)}, u32[]{:S(2)}) collective-permute-start(f32[16,128]{1,0:T(8,128)S(1)} %concatenate.41), channel_id=1, source_target_pairs={{0,64},{64,0},{1,65},{65,1},{2,66},{66,2},{3,67},{67,3},{4,68},{68... | collective-permute-start | bytes 24584 | tf_op jit(solution)/shard_map/ppermute | solution.py:264
  27.1 6.4 %collective-permute-done = f32[16,128]{1,0:T(8,128)S(1)} collective-permute-done((f32[16,128]{1,0:T(8,128)S(1)}, f32[16,128]{1,0:T(8,128)S(1)}, u32[]{:S(2)}, u32[]{:S(2)}) %collective-permute-start) | collective-permute-done | bytes 8224 | tf_op jit(solution)/shard_map/ppermute | solution.py:264
  33.5 1.3 %collective-permute-start.1 = (f32[2,16,128]{2,1,0:T(8,128)S(1)}, f32[2,16,128]{2,1,0:T(8,128)S(1)}, u32[]{:S(2)}, u32[]{:S(2)}) collective-permute-start(f32[2,16,128]{2,1,0:T(8,128)S(1)} %pad_maximum_fusion), channel_id=1, source_target_pairs={{0,128},{64,192},{1,129},{65,193},{2,130},{66,194},{3,131},{67,195... | collective-permute-start | bytes 49160 | tf_op jit(solution)/shard_map/ppermute | solution.py:266
  34.8 1.3 %collective-permute-start.3 = (f32[16,128]{1,0:T(8,128)S(1)}, f32[16,128]{1,0:T(8,128)S(1)}, u32[]{:S(2)}, u32[]{:S(2)}) collective-permute-start(f32[16,128]{1,0:T(8,128)S(1)} %concatenate.41), channel_id=1, source_target_pairs={{192,0},{128,64},{193,1},{129,65},{194,2},{130,66},{195,3},{131,67... | collective-permute-start | bytes 24584 | tf_op jit(solution)/shard_map/ppermute | solution.py:263
  36.1 0.7 collective-permute-start.2
  36.8 1.3 %collective-permute-start.4 = (f32[16,128]{1,0:T(8,128)S(1)}, f32[16,128]{1,0:T(8,128)S(1)}, u32[]{:S(2)}, u32[]{:S(2)}) collective-permute-start(f32[16,128]{1,0:T(8,128)S(1)} %concatenate.41), channel_id=1, source_target_pairs={{128,0},{192,64},{129,1},{193,65},{130,2},{194,66},{131,3},{195,67... | collective-permute-start | bytes 24584 | tf_op jit(solution)/shard_map/ppermute | solution.py:262
  38.1 5.0 %collective-permute-done.3 = f32[16,128]{1,0:T(8,128)S(1)} collective-permute-done((f32[16,128]{1,0:T(8,128)S(1)}, f32[16,128]{1,0:T(8,128)S(1)}, u32[]{:S(2)}, u32[]{:S(2)}) %collective-permute-start.3) | collective-permute-done | bytes 8224 | tf_op jit(solution)/shard_map/ppermute | solution.py:263
  43.1 0.0 collective-permute-done.2
  43.1 8.3 %collective-permute-done.4 = f32[16,128]{1,0:T(8,128)S(1)} collective-permute-done((f32[16,128]{1,0:T(8,128)S(1)}, f32[16,128]{1,0:T(8,128)S(1)}, u32[]{:S(2)}, u32[]{:S(2)}) %collective-permute-start.4) | collective-permute-done | bytes 8224 | tf_op jit(solution)/shard_map/ppermute | solution.py:262
  51.4 0.0 collective-permute-done.1
  51.5 6.1 %all_to_all.15 = f32[4,16,128]{2,1,0:T(8,128)S(1)} all-to-all(f32[4,16,128]{2,1,0:T(8,128)S(1)} %broadcast_in_dim.81), channel_id=1, replica_groups={{768,512,256,0},{769,513,257,1},{770,514,258,2},{771,515,259,3},{772,51..., dimensions={0} | all-to-all | bytes 65536 | tf_op jit(solution)/shard_map/all_to_all | solution.py:257
  57.7 0.1 concatenate.43
  57.8 11.4 %all_to_all.16.carried = f32[8,16,128]{2,1,0:T(8,128)S(1)} all-to-all(f32[8,16,128]{2,1,0:T(8,128)S(1)} %concatenate.43), channel_id=1, replica_groups={{56,48,40,32,24,16,8,0},{57,49,41,33,25,17,9,1},{58,50,42,34,26,18,10,2..., dimensions={0} | all-to-all | bytes 131072 | tf_op jit(solution)/shard_map/all_to_all | solution.py:257
  69.2 1.8 %finish.1 = (bf16[128,1024]{1,0:T(8,128)(2,1)}, bf16[128,1024]{1,0:T(8,128)(2,1)}, bf16[128,1024]{1,0:T(8,128)(2,1)}, bf16[128,1024]{1,0:T(8,128)(2,1)}, f32[4,1024]{1,0:T(4,128)}, /*index=5*/f32[1,1024]{1,0:T(1,128)}) custom-call(bf16[128,1024]{1,0:T(8,128)(2,1)S(1)} %get-tuple-element.52.query, bf16[128,1024]{1,0:T(8,128)(2,1)S(1)} %get-tuple-element.53.key, ...), custom_call_target="tpu_custom_call" | custom-call | tf_op jit(solution)/shard_map/finish/pallas_call | solution.py:385
  (45 shorter events, 0.4 us)
Async XLA Ops:
  3.6 21.3 %all-to-all-start = ((f32[8,16,128]{2,1,0:T(8,128)}), f32[8,16,128]{2,1,0:T(8,128)S(1)}, u32[]{:S(2)}, u32[]{:S(2)}) async-start(f32[8,16,128]{2,1,0:T(8,128)} %get-tuple-element.56), calls=%async_computation | async-start | bytes 131072 | tf_op jit(solution)/shard_map/all_to_all | solution.py:257
  22.2 0.7 copy-start.2
  22.2 0.7 %copy-start = (f32[4,1024]{1,0:T(4,128)S(1)}, f32[4,1024]{1,0:T(4,128)}, u32[]{:S(2)}) copy-start(f32[4,1024]{1,0:T(4,128)} %decay.3) | copy-start | bytes 49156
  22.2 0.7 %copy-start.1 = (f32[4,1024]{1,0:T(4,128)S(1)}, f32[4,1024]{1,0:T(4,128)}, u32[]{:S(2)}) copy-start(f32[4,1024]{1,0:T(4,128)} %residue.3) | copy-start | bytes 49156
  25.2 8.3 %collective-permute-start = (f32[16,128]{1,0:T(8,128)S(1)}, f32[16,128]{1,0:T(8,128)S(1)}, u32[]{:S(2)}, u32[]{:S(2)}) collective-permute-start(f32[16,128]{1,0:T(8,128)S(1)} %concatenate.41), channel_id=1, source_target_pairs={{0,64},{64,0},{1,65},{65,1},{2,66},{66,2},{3,67},{67,3},{4,68},{68... | collective-permute-start | bytes 24584 | tf_op jit(solution)/shard_map/ppermute | solution.py:264
  33.5 17.9 %collective-permute-start.1 = (f32[2,16,128]{2,1,0:T(8,128)S(1)}, f32[2,16,128]{2,1,0:T(8,128)S(1)}, u32[]{:S(2)}, u32[]{:S(2)}) collective-permute-start(f32[2,16,128]{2,1,0:T(8,128)S(1)} %pad_maximum_fusion), channel_id=1, source_target_pairs={{0,128},{64,192},{1,129},{65,193},{2,130},{66,194},{3,131},{67,195... | collective-permute-start | bytes 49160 | tf_op jit(solution)/shard_map/ppermute | solution.py:266
  34.8 8.3 %collective-permute-start.3 = (f32[16,128]{1,0:T(8,128)S(1)}, f32[16,128]{1,0:T(8,128)S(1)}, u32[]{:S(2)}, u32[]{:S(2)}) collective-permute-start(f32[16,128]{1,0:T(8,128)S(1)} %concatenate.41), channel_id=1, source_target_pairs={{192,0},{128,64},{193,1},{129,65},{194,2},{130,66},{195,3},{131,67... | collective-permute-start | bytes 24584 | tf_op jit(solution)/shard_map/ppermute | solution.py:263
  36.1 7.0 %collective-permute-start.2 = (f32[16,128]{1,0:T(8,128)S(1)}, f32[16,128]{1,0:T(8,128)S(1)}, u32[]{:S(2)}, u32[]{:S(2)}) collective-permute-start(f32[16,128]{1,0:T(8,128)S(1)} %concatenate.41), channel_id=1, source_target_pairs={{128,192},{192,128},{129,193},{193,129},{130,194},{194,130},{131,1... | collective-permute-start | bytes 24584 | tf_op jit(solution)/shard_map/ppermute | solution.py:267
  36.8 14.6 %collective-permute-start.4 = (f32[16,128]{1,0:T(8,128)S(1)}, f32[16,128]{1,0:T(8,128)S(1)}, u32[]{:S(2)}, u32[]{:S(2)}) collective-permute-start(f32[16,128]{1,0:T(8,128)S(1)} %concatenate.41), channel_id=1, source_target_pairs={{128,0},{192,64},{129,1},{193,65},{130,2},{194,66},{131,3},{195,67... | collective-permute-start | bytes 24584 | tf_op jit(solution)/shard_map/ppermute | solution.py:262

commit v5 on v3

--- a/solution.py
+++ b/solution.py
@@ -12,6 +12,7 @@
 SEGS = 8
 LANES = 128
 TOGETHER = 2
+LEAD = 4
 MIX_WIDTH = 512
 VMEM_LIMIT = 16 * 1024 * 1024
 
@@ -252,8 +253,8 @@
     return jnp.concatenate([*parts, rest], axis=-2)
 
 
-def exchanged(blocks, axis):
-    return lax.all_to_all(blocks, axis, 0, 0, tiled=True)
+def exchanged(blocks, axis, order):
+    return lax.all_to_all(blocks, axis, 0, 0, tiled=True, axis_index_groups=[order])
 
 
 def swapped(block, place):
@@ -308,7 +309,10 @@
     )(*sources, decay, residue, skip[None, :])
 
     near = ("z_lo", "core")
-    own_decay = lax.dynamic_index_in_dim(decays, lax.axis_index(near), 0, False)
+    near_count = lax.axis_size(near)
+    near_order = [(i + LEAD) % near_count for i in range(near_count)]
+    own_chunk = lax.rem(lax.axis_index(near) + near_count - LEAD, near_count)
+    own_decay = lax.dynamic_index_in_dim(decays, own_chunk, 0, False)
     log_decay = jnp.log1p(own_decay - 1.0)
 
     def power(counts):
@@ -317,12 +321,11 @@
     def held(used, counts):
         return jnp.where(used[:, None, None], power(jnp.maximum(counts, 0).astype(f32)), 0.0)
 
-    near_count = lax.axis_size(near)
     mid_count, far_count = lax.axis_size("z_hi"), lax.axis_size("y")
     mid_place, far_place = lax.axis_index("z_hi"), lax.axis_index("y")
     mid_length = tokens * near_count
     far_length = mid_length * mid_count
-    near_place = jnp.arange(near_count)
+    near_place = (jnp.arange(near_count) + LEAD) % near_count
     reach_in = power((tokens * near_place).astype(f32))
     reach_back = power((tokens * (near_count - 1 - near_place)).astype(f32))
     doublings = (near_count * mid_count * far_count).bit_length() - 1
@@ -339,9 +342,10 @@
     spread = jnp.sqrt((1.0 - own_decay) * (1.0 + own_decay)) * scale
 
     def shared(stretch, count, axis):
-        return parts_of(exchanged(jnp.broadcast_to(padded(stretch)[None], (count, 4 * MODES, LANES)), axis))
-
-    near_parts = exchanged(summary, near)
+        blocks = jnp.broadcast_to(padded(stretch)[None], (count, 4 * MODES, LANES))
+        return parts_of(exchanged(blocks, axis, list(reversed(range(count))))[::-1])
+
+    near_parts = exchanged(summary, near, near_order)
     (
         near_parts, forward, backward, entered, left, own_decay, spread,
         reach_in, reach_back, spans, mid_in, mid_back, far_in, far_back,
@@ -352,13 +356,14 @@
         )
     )
     near_spans, mid_spans, far_spans = spans[:near_steps], spans[near_steps:mid_steps], spans[mid_steps:]
-    parts = parts_of(near_parts)
+    parts = parts_of(jnp.roll(near_parts, LEAD, axis=0))
     ahead, behind = running(parts[0], near_spans, False), running(parts[1], near_spans, True)
     rest = jnp.zeros((1, MODES, LANES), f32)
     near_before = jnp.concatenate([rest, ahead[:-1]], axis=0)
     near_after = jnp.concatenate([behind[1:], rest], axis=0)
     products = jnp.sum(parts[2] + own_decay * parts[1] * near_before, axis=0)
     stretch = (ahead[-1], behind[0], products, jnp.sum(parts[3], axis=0))
+    near_before, near_after = jnp.roll(near_before, -LEAD, axis=0), jnp.roll(near_after, -LEAD, axis=0)
     near_before, near_after, stretch = lax.optimization_barrier((near_before, near_after, stretch))
     parts = parts_of(jnp.stack(swapped(padded(stretch), mid_place)))
     entering, leaving = weighted(mid_in, parts[0]), weighted(mid_back, parts[1])
@@ -377,7 +382,7 @@
             jnp.broadcast_to(scale * plain, (near_count, 1, LANES)),
         )
     )
-    carried = exchanged(carried, near)
+    carried = exchanged(carried, near, near_order)
 
     bf16 = shape_of((tokens, width), query.dtype)
     *grads, skip_grad = pl.pallas_call(

time: 74.4 us -> 71.4 us (0.960)
  waiting for transfers between devices: 22.3 us -> 20.4 us
  blocking collectives: 19.2 us -> 17.5 us
    all_to_all x1, waiting for transfers between devices: 2.72 us -> 0.68 us  [exchanged(): lax.all_to_all(blocks, axis, 0, 0, tiled=True, axis_index_groups=[order])]
    all_to_all x2, blocking collectives: 19.2 us -> 17.5 us  [exchanged(): lax.all_to_all(blocks, axis, 0, 0, tiled=True, axis_index_groups=[order])]
where the time goes in v5:
time: 71.4 us; the launch traced here: 70.8 us
  starting transfers between devices  24.4 us (34%)
  waiting for transfers between devices  20.4 us (29%)
  blocking collectives  17.5 us (25%)
  Pallas kernels  5.94 us (8%)
  between operations  1.06 us (1%)
  local copies, waits for them, and re-layouts  0.94 us (1%)
    all_to_all x1, starting transfers between devices, exchanged(): lax.all_to_all(blocks, axis, 0, 0, tiled=True, axis_index_groups=[order])  17.9 us
    all_to_all x2, blocking collectives, exchanged(): lax.all_to_all(blocks, axis, 0, 0, tiled=True, axis_index_groups=[order])  17.5 us
    ppermute x1, waiting for transfers between devices, swapped(): across = lax.ppermute(block, 'z_hi', [(2, 0), (3, 1)])  8.28 us
    ppermute x1, waiting for transfers between devices, swapped(): low = lax.ppermute(block, 'z_hi', [(0, 1), (1, 0)])  6.36 us
    ppermute x1, waiting for transfers between devices, swapped(): wrapped = lax.ppermute(block, 'z_hi', [(3, 0), (2, 1)])  5.05 us
    pallas_call x1, Pallas kernels, local(): pl.pallas_call(summarize, in_specs=[far_off] * 5, out_specs=[whole] * 5,...  2.96 us
    ppermute x1, starting transfers between devices, swapped(): low = lax.ppermute(block, 'z_hi', [(0, 1), (1, 0)])  1.91 us
    pallas_call x1, Pallas kernels, local(): pl.pallas_call(finish, grid=grid, in_specs=[wide] * 4 + [modes] * 2 + [pe...  1.77 us
  transfers between devices with their start and end apart: 6, of which 4 were waited for; matrix products, arithmetic and copies ran while one was open for 0% of the time, Pallas kernels for 2%

profile of v5, /device:TPU:1, one launch (start us, length us, event | category | flops | bytes accessed | tf_op | source)
XLA Modules:
  0.0 70.8 jit_solution(3904300018587788234)
XLA Ops:
  0.6 3.0 %summarize.1 = (f32[8,16,128]{2,1,0:T(8,128)}, bf16[128,1024]{1,0:T(8,128)(2,1)S(1)}, bf16[128,1024]{1,0:T(8,128)(2,1)S(1)}, bf16[128,1024]{1,0:T(8,128)(2,1)S(1)}, bf16[128,1024]{1,0:T(8,128)(2,1)S(1)}) custom-call(bf16[128,1024]{1,0:T(8,128)(2,1)} %query.1, bf16[128,1024]{1,0:T(8,128)(2,1)} %key.1, bf16[128,1024]{1,0:T(8,128)(2,1)} %value.1, ...), custom_call_target="tpu_custom_call" | custom-call | tf_op jit(solution)/shard_map/summarize/pallas_call | solution.py:287
  3.6 17.9 %all-to-all-start = ((f32[8,16,128]{2,1,0:T(8,128)}), f32[8,16,128]{2,1,0:T(8,128)S(1)}, u32[]{:S(2)}, u32[]{:S(2)}) async-start(f32[8,16,128]{2,1,0:T(8,128)} %get-tuple-element.56), calls=%async_computation | async-start | bytes 131072 | tf_op jit(solution)/shard_map/all_to_all | solution.py:257
  21.6 0.0 copy-start.2
  21.6 0.0 copy-start
  21.6 0.0 copy-start.1
  21.6 0.6 copy-done.2
  22.3 0.0 copy-done
  22.3 0.0 copy-done.1
  22.3 1.2 %mix.1 = (f32[16,8,1024]{2,1,0:T(8,128)S(1)}, f32[16,8,1024]{2,1,0:T(8,128)S(1)}, f32[4,8,1024]{2,1,0:T(8,128)S(1)}, f32[4,8,1024]{2,1,0:T(8,128)S(1)}, f32[8,4,128]{2,1,0:T(4,128)S(1)}) custom-call(bf16[128,1024]{1,0:T(8,128)(2,1)S(1)} %get-tuple-element.52.query, bf16[128,1024]{1,0:T(8,128)(2,1)S(1)} %get-tuple-element.53.key, ...), custom_call_target="tpu_custom_call" | custom-call | flops 5242880 | bytes 2097152 | tf_op jit(solution)/shard_map/mix/pallas_call | solution.py:298
  23.6 0.1 multiply_exponential_fusion.2
  23.7 0.1 multiply_exponential_fusion
  23.8 0.1 exponential_select_fusion
  23.9 0.7 all-to-all-done
  25.0 1.9 %collective-permute-start = (f32[16,128]{1,0:T(8,128)S(1)}, f32[16,128]{1,0:T(8,128)S(1)}, u32[]{:S(2)}, u32[]{:S(2)}) collective-permute-start(f32[16,128]{1,0:T(8,128)S(1)} %concatenate.55), channel_id=1, source_target_pairs={{0,64},{64,0},{1,65},{65,1},{2,66},{66,2},{3,67},{67,3},{4,68},{68... | collective-permute-start | bytes 24584 | tf_op jit(solution)/shard_map/ppermute | solution.py:264
  26.9 6.4 %collective-permute-done = f32[16,128]{1,0:T(8,128)S(1)} collective-permute-done((f32[16,128]{1,0:T(8,128)S(1)}, f32[16,128]{1,0:T(8,128)S(1)}, u32[]{:S(2)}, u32[]{:S(2)}) %collective-permute-start) | collective-permute-done | bytes 8224 | tf_op jit(solution)/shard_map/ppermute | solution.py:264
  33.3 1.3 %collective-permute-start.1 = (f32[2,16,128]{2,1,0:T(8,128)S(1)}, f32[2,16,128]{2,1,0:T(8,128)S(1)}, u32[]{:S(2)}, u32[]{:S(2)}) collective-permute-start(f32[2,16,128]{2,1,0:T(8,128)S(1)} %pad_maximum_fusion.2), channel_id=1, source_target_pairs={{0,128},{64,192},{1,129},{65,193},{2,130},{66,194},{3,131},{67,195... | collective-permute-start | bytes 49160 | tf_op jit(solution)/shard_map/ppermute | solution.py:266
  34.5 1.3 %collective-permute-start.3 = (f32[16,128]{1,0:T(8,128)S(1)}, f32[16,128]{1,0:T(8,128)S(1)}, u32[]{:S(2)}, u32[]{:S(2)}) collective-permute-start(f32[16,128]{1,0:T(8,128)S(1)} %concatenate.55), channel_id=1, source_target_pairs={{192,0},{128,64},{193,1},{129,65},{194,2},{130,66},{195,3},{131,67... | collective-permute-start | bytes 24584 | tf_op jit(solution)/shard_map/ppermute | solution.py:263
  35.8 0.7 collective-permute-start.2
  36.5 1.3 %collective-permute-start.4 = (f32[16,128]{1,0:T(8,128)S(1)}, f32[16,128]{1,0:T(8,128)S(1)}, u32[]{:S(2)}, u32[]{:S(2)}) collective-permute-start(f32[16,128]{1,0:T(8,128)S(1)} %concatenate.55), channel_id=1, source_target_pairs={{128,0},{192,64},{129,1},{193,65},{130,2},{194,66},{131,3},{195,67... | collective-permute-start | bytes 24584 | tf_op jit(solution)/shard_map/ppermute | solution.py:262
  37.8 5.0 %collective-permute-done.3 = f32[16,128]{1,0:T(8,128)S(1)} collective-permute-done((f32[16,128]{1,0:T(8,128)S(1)}, f32[16,128]{1,0:T(8,128)S(1)}, u32[]{:S(2)}, u32[]{:S(2)}) %collective-permute-start.3) | collective-permute-done | bytes 8224 | tf_op jit(solution)/shard_map/ppermute | solution.py:263
  42.9 0.0 collective-permute-done.2
  42.9 8.3 %collective-permute-done.4 = f32[16,128]{1,0:T(8,128)S(1)} collective-permute-done((f32[16,128]{1,0:T(8,128)S(1)}, f32[16,128]{1,0:T(8,128)S(1)}, u32[]{:S(2)}, u32[]{:S(2)}) %collective-permute-start.4) | collective-permute-done | bytes 8224 | tf_op jit(solution)/shard_map/ppermute | solution.py:262
  51.2 0.0 collective-permute-done.1
  51.3 6.3 %all_to_all.15 = f32[4,16,128]{2,1,0:T(8,128)S(1)} all-to-all(f32[4,16,128]{2,1,0:T(8,128)S(1)} %broadcast_in_dim.81), channel_id=1, replica_groups={{768,512,256,0},{769,513,257,1},{770,514,258,2},{771,515,259,3},{772,51..., dimensions={0} | all-to-all | bytes 65536 | tf_op jit(solution)/shard_map/all_to_all | solution.py:257
  57.7 0.1 concatenate.57
  57.8 11.2 %all_to_all.16.carried = f32[8,16,128]{2,1,0:T(8,128)S(1)} all-to-all(f32[8,16,128]{2,1,0:T(8,128)S(1)} %concatenate.57), channel_id=1, replica_groups={{32,40,48,56,0,8,16,24},{33,41,49,57,1,9,17,25},{34,42,50,58,2,10,18,26..., dimensions={0} | all-to-all | bytes 131072 | tf_op jit(solution)/shard_map/all_to_all | solution.py:257
  69.0 1.8 %finish.1 = (bf16[128,1024]{1,0:T(8,128)(2,1)}, bf16[128,1024]{1,0:T(8,128)(2,1)}, bf16[128,1024]{1,0:T(8,128)(2,1)}, bf16[128,1024]{1,0:T(8,128)(2,1)}, f32[4,1024]{1,0:T(4,128)}, /*index=5*/f32[1,1024]{1,0:T(1,128)}) custom-call(bf16[128,1024]{1,0:T(8,128)(2,1)S(1)} %get-tuple-element.52.query, bf16[128,1024]{1,0:T(8,128)(2,1)S(1)} %get-tuple-element.53.key, ...), custom_call_target="tpu_custom_call" | custom-call | tf_op jit(solution)/shard_map/finish/pallas_call | solution.py:388
  (51 shorter events, 0.5 us)
Async XLA Ops:
  3.6 21.0 %all-to-all-start = ((f32[8,16,128]{2,1,0:T(8,128)}), f32[8,16,128]{2,1,0:T(8,128)S(1)}, u32[]{:S(2)}, u32[]{:S(2)}) async-start(f32[8,16,128]{2,1,0:T(8,128)} %get-tuple-element.56), calls=%async_computation | async-start | bytes 131072 | tf_op jit(solution)/shard_map/all_to_all | solution.py:257
  21.6 0.7 copy-start.2
  21.6 0.7 %copy-start = (f32[4,1024]{1,0:T(4,128)S(1)}, f32[4,1024]{1,0:T(4,128)}, u32[]{:S(2)}) copy-start(f32[4,1024]{1,0:T(4,128)} %decay.3) | copy-start | bytes 49156
  21.6 0.7 %copy-start.1 = (f32[4,1024]{1,0:T(4,128)S(1)}, f32[4,1024]{1,0:T(4,128)}, u32[]{:S(2)}) copy-start(f32[4,1024]{1,0:T(4,128)} %residue.3) | copy-start | bytes 49156
  25.0 8.3 %collective-permute-start = (f32[16,128]{1,0:T(8,128)S(1)}, f32[16,128]{1,0:T(8,128)S(1)}, u32[]{:S(2)}, u32[]{:S(2)}) collective-permute-start(f32[16,128]{1,0:T(8,128)S(1)} %concatenate.55), channel_id=1, source_target_pairs={{0,64},{64,0},{1,65},{65,1},{2,66},{66,2},{3,67},{67,3},{4,68},{68... | collective-permute-start | bytes 24584 | tf_op jit(solution)/shard_map/ppermute | solution.py:264
  33.3 17.9 %collective-permute-start.1 = (f32[2,16,128]{2,1,0:T(8,128)S(1)}, f32[2,16,128]{2,1,0:T(8,128)S(1)}, u32[]{:S(2)}, u32[]{:S(2)}) collective-permute-start(f32[2,16,128]{2,1,0:T(8,128)S(1)} %pad_maximum_fusion.2), channel_id=1, source_target_pairs={{0,128},{64,192},{1,129},{65,193},{2,130},{66,194},{3,131},{67,195... | collective-permute-start | bytes 49160 | tf_op jit(solution)/shard_map/ppermute | solution.py:266
  34.5 8.3 %collective-permute-start.3 = (f32[16,128]{1,0:T(8,128)S(1)}, f32[16,128]{1,0:T(8,128)S(1)}, u32[]{:S(2)}, u32[]{:S(2)}) collective-permute-start(f32[16,128]{1,0:T(8,128)S(1)} %concatenate.55), channel_id=1, source_target_pairs={{192,0},{128,64},{193,1},{129,65},{194,2},{130,66},{195,3},{131,67... | collective-permute-start | bytes 24584 | tf_op jit(solution)/shard_map/ppermute | solution.py:263
  35.8 7.0 %collective-permute-start.2 = (f32[16,128]{1,0:T(8,128)S(1)}, f32[16,128]{1,0:T(8,128)S(1)}, u32[]{:S(2)}, u32[]{:S(2)}) collective-permute-start(f32[16,128]{1,0:T(8,128)S(1)} %concatenate.55), channel_id=1, source_target_pairs={{128,192},{192,128},{129,193},{193,129},{130,194},{194,130},{131,1... | collective-permute-start | bytes 24584 | tf_op jit(solution)/shard_map/ppermute | solution.py:267
  36.5 14.6 %collective-permute-start.4 = (f32[16,128]{1,0:T(8,128)S(1)}, f32[16,128]{1,0:T(8,128)S(1)}, u32[]{:S(2)}, u32[]{:S(2)}) collective-permute-start(f32[16,128]{1,0:T(8,128)S(1)} %concatenate.55), channel_id=1, source_target_pairs={{128,0},{192,64},{129,1},{193,65},{130,2},{194,66},{131,3},{195,67... | collective-permute-start | bytes 24584 | tf_op jit(solution)/shard_map/ppermute | solution.py:262
